TPU v7x, 1024 devices: a whole 8x8x8 slice. The times are simulated.
1024 devices in a mesh: lat: 16 (over z, core), lon: 64 (over y, x).
Axes of the slice: x: 8, y: 8, z: 8, core: 2. Of those that a mesh axis runs over, the one named last changes fastest.
Arguments:
- field: bfloat16 [16, 10616832], P(None, ('lat', 'lon')), may hold values from -6 to 6
- dep_frac: float32 [10616832], P(('lat', 'lon')), may hold values from 0 to 1
- dep_index: int32 [2, 10616832], P(None, ('lat', 'lon')), may hold values from 0 to 11663, as said below
- send_list: int32 [1024, 2, 8], P(('lat', 'lon')), may hold values from 0 to 128, as said below
- send_count: int32 [1024, 2], P(('lat', 'lon')), may hold values from 0 to 8, as said below
- cycle_len: int32 [16, 128], P('lat'), may hold values from 20 to 5136, as said below
- diffusion: float32 [16], replicated, may hold values from 0.1 to 10
Outputs:
- smoothed: bfloat16 [16, 10616832], P(None, ('lat', 'lon'))
Inputs may be any that keep to these rules, and one draw needn't show every extreme that they name: `cycle_len`: every circle length is 4 j + 16 for a whole number j. `send_count`: counts of used list entries; some device uses all 8. `send_list`: the used entries of a list are distinct circle numbers below 128; every unused entry is 128. `dep_index`: positions in the column's own device's extended list of 11664 columns; row 1 is row 0 plus one.
All inputs are finite; a program needn't handle non-finite values.
Results may differ from a plain program's by a relative error of at most 0.0049.
Values may be sent and summed in bfloat16 or wider, within the bound.
No kernel may reach another device: no remote copies, remote signals or barrier semaphores. Data moves between devices by JAX's collectives and lax.ppermute only.
A program may use at most 32 MiB of HBM per device.

v0:
```python
import math

import jax
import jax.numpy as jnp
from jax import lax
from jax.sharding import PartitionSpec as P

TRUNC = 640
HALO_BLOCKS = 8


def extended_2(cells, sides, width):
    for axis, dim in sides:
        count = lax.axis_size(axis)
        ends = count - 1
        head = lax.slice_in_dim(cells, 0, width, axis=dim)
        tail = lax.slice_in_dim(cells, cells.shape[dim] - width, cells.shape[dim], axis=dim)
        cells = jnp.concatenate(
            [
                lax.ppermute(tail, axis, [(i, (i + 1) % count) for i in range(ends)]),
                cells,
                lax.ppermute(head, axis, [((i + 1) % count, i) for i in range(ends)]),
            ],
            axis=dim,
        )
    return cells


def spectral_weights(wavenumber_index, length, length_real, diffusion):
    ratio = wavenumber_index.astype(jnp.float32) / TRUNC
    weight = jnp.where((wavenumber_index == 0) | (2 * wavenumber_index == length), 1.0, 2.0)
    weight = jnp.where(2 * wavenumber_index <= length, weight, 0.0)
    return weight[None, :] / (
        (1.0 + diffusion[:, None] * ratio[None, :] * ratio[None, :]) * length_real
    )


def cycle_filter(cycle_data, length, diffusion, longitude_count):
    channels, lon_sets, slot_count = cycle_data.shape
    width = min(128, TRUNC)
    field_values = cycle_data.astype(jnp.float32)
    length_real = length.astype(jnp.float32)
    angle_scale = 2.0 * math.pi / length_real
    slot_start = jnp.arange(slot_count, dtype=jnp.int32) * longitude_count
    lon_place = jnp.arange(lon_sets, dtype=jnp.int32)
    needed = (jnp.minimum(TRUNC, length // 2 + 1) + width - 1) // width

    def one_block(number, summed):
        wavenumber_index = number * width + jnp.arange(width, dtype=jnp.int32)
        slot_phase = wavenumber_index[None, :] * slot_start[:, None] % length
        lon_phase = wavenumber_index[None, :] * lon_place[:, None] % length
        slot_longitude_angle = slot_phase.astype(jnp.float32) * angle_scale
        lon_angle = lon_phase.astype(jnp.float32) * angle_scale
        slot_lookup_table = jnp.concatenate(
            [jnp.cos(slot_longitude_angle), jnp.sin(slot_longitude_angle)], axis=1
        )
        lon_cosine = jnp.cos(lon_angle)
        lon_sine = jnp.sin(lon_angle)
        partial_terms = jnp.einsum(
            "foh,hq->foq", field_values, slot_lookup_table, precision=lax.Precision.HIGHEST
        )
        slot_cosine = partial_terms[:, :, :width]
        slot_sine = partial_terms[:, :, width:]
        coeff_cos = jnp.sum(lon_cosine[None] * slot_cosine - lon_sine[None] * slot_sine, axis=1)
        coeff_sin = jnp.sum(lon_sine[None] * slot_cosine + lon_cosine[None] * slot_sine, axis=1)
        damping = spectral_weights(wavenumber_index, length, length_real, diffusion)
        amp_cos = (coeff_cos * damping)[:, None, :]
        amp_sin = (coeff_sin * damping)[:, None, :]
        cos_part = amp_cos * lon_cosine[None] + amp_sin * lon_sine[None]
        sin_part = amp_sin * lon_cosine[None] - amp_cos * lon_sine[None]
        stacked_fields = jnp.concatenate([cos_part, sin_part], axis=2)
        return summed + jnp.einsum(
            "fat,ut->fau", stacked_fields, slot_lookup_table, precision=lax.Precision.HIGHEST
        )

    summed = lax.fori_loop(
        0, needed, one_block, jnp.zeros((channels, lon_sets, slot_count), jnp.float32)
    )
    cycle_point = slot_start[None, :] + lon_place[:, None]
    return jnp.where(cycle_point[None] < length, summed, 0.0)


def on_device(field, dep_frac, dep_index, send_list, send_count, cycle_len, diffusion):
    longitude_count = lax.axis_size("lon")
    lon_index = lax.axis_index("lon")
    channels, own_cols = field.shape
    lengths = cycle_len[0]
    cycle_count = lengths.shape[0]
    slot_count = own_cols // cycle_count
    slot_points = jnp.arange(slot_count, dtype=jnp.int32) * longitude_count + lon_index
    validity_mask = (slot_points[None, :] < lengths[:, None]).reshape(-1)
    masked = jnp.where(validity_mask[None, :], field, jnp.zeros_like(field))
    cycle_blocks = masked.reshape(channels, cycle_count, slot_count)
    chosen = jnp.clip(send_list.reshape(-1), 0, cycle_count - 1)
    kept_mask = (
        jnp.arange(HALO_BLOCKS, dtype=jnp.int32)[None, :] < send_count.reshape(2)[:, None]
    ).reshape(-1)
    picked = jnp.take(cycle_blocks, chosen, axis=1)
    picked = jnp.where(kept_mask[None, :, None], picked, jnp.zeros_like(picked))
    outgoing = picked.reshape(channels, 2 * HALO_BLOCKS * slot_count)
    rim_width = HALO_BLOCKS * slot_count
    arrived = extended_2(outgoing, (("lat", 1),), rim_width)
    extended = jnp.concatenate(
        [masked, arrived[:, :rim_width], arrived[:, 3 * rim_width :]], axis=1
    )
    lower_value = jnp.take(extended, dep_index[0], axis=1).astype(jnp.float32)
    upper_value = jnp.take(extended, dep_index[1], axis=1).astype(jnp.float32)
    blended = (1.0 - dep_frac)[None, :] * lower_value + dep_frac[None, :] * upper_value
    departed = jnp.where(validity_mask[None, :], blended, 0.0).astype(jnp.bfloat16)
    per_owner = cycle_count // longitude_count
    cycle_major = departed.reshape(channels, cycle_count, slot_count)
    placing = jnp.arange(cycle_count, dtype=jnp.int32)
    received = lax.all_to_all(
        cycle_major.reshape(channels, longitude_count, per_owner * slot_count),
        "lon",
        split_axis=1,
        concat_axis=1,
        tiled=True,
    )
    results = []
    for cycle_turn in range(per_owner):
        cycle_id = placing[lon_index * per_owner + cycle_turn]
        cycle_piece = received[:, :, cycle_turn * slot_count : (cycle_turn + 1) * slot_count]
        filtered = cycle_filter(cycle_piece, lengths[cycle_id], diffusion, longitude_count)
        results.append(filtered.astype(jnp.bfloat16))
    returned = jnp.stack(results, axis=2).reshape(channels, longitude_count, per_owner * slot_count)
    landed = lax.all_to_all(returned, "lon", split_axis=1, concat_axis=1, tiled=True).reshape(
        channels, cycle_count, slot_count
    )
    return landed.reshape(channels, own_cols)


def solution(mesh):
    placed = (
        P(None, ("lat", "lon")),
        P(("lat", "lon")),
        P(None, ("lat", "lon")),
        P(("lat", "lon"), None, None),
        P(("lat", "lon"), None),
        P("lat", None),
        P(),
    )
    return jax.shard_map(
        on_device, mesh=mesh, in_specs=placed, out_specs=P(None, ("lat", "lon")), check_vma=False
    )
```

profile of v0, /device:TPU:512, one launch (start us, length us, event | category | flops | bytes accessed | tf_op | source)
XLA Modules:
  0.0 175.7 jit_solution(2320446523791836353)
XLA Ops:
  2.9 1.6 reshape.506
  6.3 1.9 %collective-permute-start = (bf16[16,648]{1,0:T(8,128)(2,1)S(1)}, bf16[16,648]{1,0:T(8,128)(2,1)S(1)}, u32[]{:S(2)}, u32[]{:S(2)}) collective-permute-start(bf16[16,648]{1,0:T(8,128)(2,1)S(1)} %get-tuple-element.463), channel_id=1, source_target_pairs={{0,64},{64,128},{128,192},{192,256},{256,320},{320,384},{384,448},... | collective-permute-start | bytes 62216 | tf_op jit(solution)/shard_map/ppermute | solution.py:20
  8.2 4.9 %collective-permute-start.1 = (bf16[16,648]{1,0:T(8,128)(2,1)S(1)}, bf16[16,648]{1,0:T(8,128)(2,1)S(1)}, u32[]{:S(2)}, u32[]{:S(2)}) collective-permute-start(bf16[16,648]{1,0:T(8,128)(2,1)S(1)} %get-tuple-element.462), channel_id=1, source_target_pairs={{64,0},{128,64},{192,128},{256,192},{320,256},{384,320},{448,384},... | collective-permute-start | bytes 62216 | tf_op jit(solution)/shard_map/ppermute | solution.py:22
  14.7 2.6 %copy.63 = bf16[16,11664]{0,1:T(8,128)(2,1)S(1)} copy(bf16[16,11664]{1,0:T(8,128)(2,1)S(1)} %concatenate.23) | data formatting | bytes 746496 | tf_op jit(solution)/shard_map/concatenate | solution.py:103
  17.3 21.9 %gather_fusion.1 = bf16[10368,16]{1,0:T(8,128)(2,1)} fusion(bf16[16,11664]{0,1:T(8,128)(2,1)S(1)} %copy.63, s32[11264]{0:T(1024)S(1)} %pad_clamp_fusion.1), kind=kCustom, calls=%fused_computation.clone | custom fusion | bytes 705024 | tf_op jit(solution)/shard_map/jit(_take)/gather | solution.py:106
  39.2 2.4 %copy.64 = bf16[10368,16]{0,1:T(8,128)(2,1)S(1)} copy(bf16[10368,16]{1,0:T(8,128)(2,1)} %gather_fusion.1) | data formatting | bytes 663552 | tf_op jit(solution)/shard_map/jit(_take)/gather | solution.py:106
  41.6 21.9 %gather_fusion.2 = bf16[10368,16]{1,0:T(8,128)(2,1)} fusion(bf16[16,11664]{0,1:T(8,128)(2,1)S(1)} %copy.63, s32[11264]{0:T(1024)S(1)} %pad_clamp_fusion), kind=kCustom, calls=%fused_computation.1.clone | custom fusion | bytes 705024 | tf_op jit(solution)/shard_map/jit(_take)/gather | solution.py:107
  63.4 2.4 %copy.66 = bf16[10368,16]{0,1:T(8,128)(2,1)S(1)} copy(bf16[10368,16]{1,0:T(8,128)(2,1)} %gather_fusion.2) | data formatting | bytes 663552 | tf_op jit(solution)/shard_map/jit(_take)/gather | solution.py:107
  66.1 1.5 reshape_reshape.6
  68.7 13.5 %all-to-all-start = ((bf16[16,64,162]{2,0,1:T(8,128)(2,1)}), bf16[16,64,162]{2,0,1:T(8,128)(2,1)S(1)}, u32[]{:S(2)}, u32[]{:S(2)}) async-start(bf16[16,64,162]{2,0,1:T(8,128)(2,1)} %copy.67), calls=%async_computation | async-start | bytes 1048576 | tf_op jit(solution)/shard_map/all_to_all | solution.py:113
  91.2 1.2 fusion.59
  92.4 9.6 %all-to-all-done = bf16[16,64,162]{2,0,1:T(8,128)(2,1)S(1)} async-done(((bf16[16,64,162]{2,0,1:T(8,128)(2,1)}), bf16[16,64,162]{2,0,1:T(8,128)(2,1)S(1)}, u32[]{:S(2)}, u32[]{:S(2)}) %all-to-all-start) | async-done | bytes 331808 | tf_op jit(solution)/shard_map/all_to_all | solution.py:113
  102.4 22.5 %while.26 = (s32[]{:T(128)}, f32[16,64,81]{2,1,0:T(8,128)S(1)}, s32[]{:T(128)}, s32[]{:T(128)}, pred[]{:T(512)}, /*index=5*/f32[]{:T(128)}, f32[16,64,81]{2,1,0:...) while((s32[]{:T(128)}, f32[16,64,81]{2,1,0:T(8,128)S(1)}, ...), condition=%wide.region_3.5_spmd.clone, body=%wide.region_0.0_spmd.clone.sunk | while | flops 512026816 | bytes 5705067 | solution.py:76
  105.7 1.1 convolution_add_fusion.4
  114.6 1.1 convolution_add_fusion.4
  119.1 1.2 convolution_add_fusion.4
  123.5 1.1 convolution_add_fusion.4
  125.1 21.9 %while.27 = (s32[]{:T(128)}, f32[16,64,81]{2,1,0:T(8,128)S(1)}, s32[]{:T(128)}, s32[]{:T(128)}, pred[]{:T(512)}, /*index=5*/f32[]{:T(128)}, f32[16,64,81]{2,1,0:...) while((s32[]{:T(128)}, f32[16,64,81]{2,1,0:T(8,128)S(1)}, ...), condition=%wide.region_7.9_spmd.clone, body=%wide.region_4.8_spmd.clone.sunk | while | flops 512026816 | bytes 5705067 | solution.py:76
  128.3 1.2 convolution_add_fusion.5
  132.7 1.1 convolution_add_fusion.5
  141.5 1.2 convolution_add_fusion.5
  145.9 1.2 convolution_add_fusion.5
  148.2 26.0 %all_to_all.10 = bf16[16,64,162]{2,0,1:T(8,128)(2,1)S(1)} all-to-all(bf16[16,64,162]{2,0,1:T(8,128)(2,1)S(1)} %reshape.540), channel_id=1, replica_groups=mesh['lat'=16,'lon'=64] {'lon'}, dimensions={1} | all-to-all | bytes 663552 | tf_op jit(solution)/shard_map/all_to_all | solution.py:127
  174.3 1.4 reshape_reshape.7
  (152 shorter events, 44.3 us)
Async XLA Ops:
  0.0 5.9 %copy-start.6 = (s32[1,2]{1,0:T(1,128)S(1)}, s32[1,2]{1,0:T(1,128)}, u32[]{:S(2)}) copy-start(s32[1,2]{1,0:T(1,128)} %param.17) | copy-start | bytes 28
  0.0 13.1 %copy-start.1 = (s32[2,10368]{1,0:T(2,128)S(1)}, s32[2,10368]{1,0:T(2,128)}, u32[]{:S(2)}) copy-start(s32[2,10368]{1,0:T(2,128)} %param.15) | copy-start | bytes 248836
  0.0 14.0 %copy-start = (f32[10368]{0:T(1024)S(1)}, f32[10368]{0:T(1024)}, u32[]{:S(2)}) copy-start(f32[10368]{0:T(1024)} %param.14) | copy-start | bytes 124420
  6.3 7.7 %collective-permute-start = (bf16[16,648]{1,0:T(8,128)(2,1)S(1)}, bf16[16,648]{1,0:T(8,128)(2,1)S(1)}, u32[]{:S(2)}, u32[]{:S(2)}) collective-permute-start(bf16[16,648]{1,0:T(8,128)(2,1)S(1)} %get-tuple-element.463), channel_id=1, source_target_pairs={{0,64},{64,128},{128,192},{192,256},{256,320},{320,384},{384,448},... | collective-permute-start | bytes 62216 | tf_op jit(solution)/shard_map/ppermute | solution.py:20
  8.2 6.4 %collective-permute-start.1 = (bf16[16,648]{1,0:T(8,128)(2,1)S(1)}, bf16[16,648]{1,0:T(8,128)(2,1)S(1)}, u32[]{:S(2)}, u32[]{:S(2)}) collective-permute-start(bf16[16,648]{1,0:T(8,128)(2,1)S(1)} %get-tuple-element.462), channel_id=1, source_target_pairs={{64,0},{128,64},{192,128},{256,192},{320,256},{384,320},{448,384},... | collective-permute-start | bytes 62216 | tf_op jit(solution)/shard_map/ppermute | solution.py:22
  41.5 24.3 %copy-start.3 = (pred[10368]{0:T(1024)(128)(4,1)S(1)}, pred[10368]{0:T(1024)(128)(4,1)}, u32[]{:S(2)}) copy-start(pred[10368]{0:T(1024)(128)(4,1)} %get-tuple-element.470) | copy-start | bytes 31108
  41.6 24.3 %copy-start.4 = (pred[10368]{0:T(1024)(128)(4,1)S(1)}, pred[10368]{0:T(1024)(128)(4,1)}, u32[]{:S(2)}) copy-start(pred[10368]{0:T(1024)(128)(4,1)} %get-tuple-element.471) | copy-start | bytes 31108
  65.8 16.4 %copy-start.5 = (s32[1,128]{1,0:T(1,128)S(1)}, s32[1,128]{1,0:T(1,128)}, u32[]{:S(2)}) copy-start(s32[1,128]{1,0:T(1,128)} %param.18) | copy-start | bytes 1540
  67.6 34.8 %copy-start.2 = (f32[16]{0:T(128)S(1)}, f32[16]{0:T(128)}, u32[]{:S(2)}) copy-start(f32[16]{0:T(128)} %param.19) | copy-start | bytes 196
  68.7 33.3 %all-to-all-start = ((bf16[16,64,162]{2,0,1:T(8,128)(2,1)}), bf16[16,64,162]{2,0,1:T(8,128)(2,1)S(1)}, u32[]{:S(2)}, u32[]{:S(2)}) async-start(bf16[16,64,162]{2,0,1:T(8,128)(2,1)} %copy.67), calls=%async_computation | async-start | bytes 1048576 | tf_op jit(solution)/shard_map/all_to_all | solution.py:113
where the time goes:
time: 176 us
  local copies, waits for them, and re-layouts  61 us (35%)
  other arithmetic  27.3 us (16%)
  blocking collectives  26 us (15%)
  matrix products  21.3 us (12%)
  starting transfers between devices  20.2 us (11%)
  waiting for transfers between devices  10.2 us (6%)
  between operations  8.73 us (5%)
    all_to_all x1, blocking collectives, on_device(): lax.all_to_all(returned, 'lon', split_axis=1, concat_axis=1, tiled=True)  26 us
    gather x2, local copies, waits for them, and re-layouts, on_device(): lower_value = jnp.take(extended, dep_index[0], axis=1).astype(jnp.float32)  24.3 us
    gather x2, local copies, waits for them, and re-layouts, on_device(): upper_value = jnp.take(extended, dep_index[1], axis=1).astype(jnp.float32)  24.3 us
    all_to_all x1, starting transfers between devices, on_device(): lax.all_to_all(cycle_major.reshape(channels, longitude_count, per_owner *...  13.5 us
    dot_general x10, matrix products, one_block(): jnp.einsum('fat,ut->fau', stacked_fields, slot_lookup_table, precision=la...  11.5 us
    dot_general x10, matrix products, one_block(): jnp.einsum('foh,hq->foq', field_values, slot_lookup_table, precision=lax....  9.82 us
    all_to_all x1, waiting for transfers between devices, on_device(): lax.all_to_all(cycle_major.reshape(channels, longitude_count, per_owner *...  9.59 us
    cos x10, other arithmetic, one_block(): jnp.cos(slot_longitude_angle)  7.21 us
  transfers between devices with their start and end apart: 3, of which 2 were waited for; matrix products, arithmetic and copies ran while one was open for 2% of the time, Pallas kernels for 0%

commit v1 on v0

v1 whole, which is shorter than its diff:
```python
import math

import jax
import jax.numpy as jnp
from jax import lax
from jax.experimental import pallas as pl
from jax.experimental.pallas import tpu as pltpu
from jax.sharding import PartitionSpec as P

TRUNC = 640
HALO_BLOCKS = 8
CH = 16
CYCLES = 128
SLOTS = 81
N_LON = 64
OWN = CYCLES * SLOTS
HALO = HALO_BLOCKS * SLOTS
LANES = 128
STRIDE = 255
WINDOW = 256
EXT = OWN + 2 * HALO
N_WIN = (EXT - 2) // STRIDE + 1
HEAD = 64
TAIL = SLOTS - HEAD
SLOT_ROWS = 96
MAIN_COLS = N_LON * LANES
K_BLOCKS = TRUNC // LANES
OWN_WIN = OWN // STRIDE + 1
RIM_OWN = OWN - STRIDE * (OWN_WIN - 1)
RIM = -(-(STRIDE * (N_WIN - OWN_WIN) + WINDOW) // LANES) * LANES
BATCH = 2 * WINDOW
MAIN_STEPS = MAIN_COLS // BATCH
FULL_STEPS = OWN // BATCH
NEAR = 4
FAR = N_LON // NEAR
F32 = jnp.float32
BF16 = jnp.bfloat16


def lane_iota(rows, cols=LANES):
    return lax.broadcasted_iota(jnp.int32, (rows, cols), 1)


def slots_used(length, lon_index):
    return (length - lon_index + (N_LON - 1)) >> 6


def pick_kernel(list_ref, count_ref, len_ref, field_ref, first_ref, second_ref):
    lon_index = lax.axis_index("lon")
    lane = lane_iota(CH, 2 * LANES)
    for way, out_ref in ((0, first_ref), (1, second_ref)):
        blocks = [jnp.zeros((CH, LANES), F32) for _ in range(7)]
        for k in range(HALO_BLOCKS):
            row = jnp.clip(list_ref[0, way, k], 0, CYCLES - 1)
            start = row * SLOTS
            base = jnp.minimum(start >> 7, OWN // LANES - 2)
            shift = start - base * LANES
            place = (SLOTS * k) % LANES
            block = (SLOTS * k) // LANES
            window = field_ref[:, pl.ds(pl.multiple_of(base * LANES, LANES), 2 * LANES)]
            moved = pltpu.roll(window.astype(F32), (place - shift + 2 * LANES) & 255, 1)
            used = jnp.where(k < count_ref[0, way], slots_used(len_ref[0, row], lon_index), 0)
            keep = (lane >= place) & (lane < place + used)
            for half in range(2):
                part = slice(half * LANES, (half + 1) * LANES)
                blocks[block + half] = jnp.where(keep[:, part], moved[:, part], blocks[block + half])
        for i in range(5):
            out_ref[:, i * LANES : (i + 1) * LANES] = blocks[i].astype(BF16)
        out_ref[:, 5 * LANES : HALO] = blocks[5][:, : HALO - 5 * LANES].astype(BF16)


def prepare_kernel(len_ref, field_ref, index_ref, frac_ref, win_ref, where_ref, ext_ref, pair_ref):
    lon_index = lax.axis_index("lon")
    pair_ref[:, OWN:] = jnp.zeros((8, LANES), F32)
    pair_ref[0:1, 0:OWN] = index_ref[0:1, :].astype(F32)
    pair_ref[1:2, 0:OWN] = frac_ref[...]
    lane = lane_iota(8)
    tile = None
    for d in range(N_LON):
        used = [slots_used(len_ref[0, 2 * d + turn], lon_index) for turn in range(2)]
        begin = 2 * SLOTS * d
        here = jnp.where(
            lane < HEAD,
            pair_ref[:, begin : begin + LANES],
            pair_ref[:, begin + TAIL : begin + TAIL + LANES],
        )
        limit = jnp.where(lane < HEAD, used[0], used[1] + HEAD)
        here = jnp.where(lane < limit, here, -1.0)
        where_ref[:, LANES * d : LANES * (d + 1)] = here[0:2]
        for turn in range(2):
            at = TAIL * (2 * d + turn)
            number, place = at // LANES, at % LANES
            source = begin + SLOTS * turn + HEAD - place
            limit = place + used[turn] - HEAD
            here = jnp.where(lane < limit, pair_ref[:, source : source + LANES], -1.0)
            tile = here if tile is None else jnp.where(lane >= place, here, tile)
            if place + TAIL >= LANES:
                column = MAIN_COLS + LANES * number
                where_ref[:, column : column + LANES] = tile[0:2]
                tile = None
                if place + TAIL > LANES:
                    source += LANES
                    tile = jnp.where(lane < limit - LANES, pair_ref[:, source : source + LANES], -1.0)

    lane = lane_iota(CH)
    for b in range(OWN // LANES):
        first = (LANES * b) // SLOTS
        last = (LANES * b + LANES - 1) // SLOTS
        limit = SLOTS * last + slots_used(len_ref[0, last], lon_index) - LANES * b
        limit = jnp.full((CH, LANES), limit, jnp.int32)
        for r in range(last - 1, first - 1, -1):
            here = SLOTS * r + slots_used(len_ref[0, r], lon_index) - LANES * b
            limit = jnp.where(lane < SLOTS * (r + 1) - LANES * b, here, limit)
        keep = jnp.where(lane < limit, 1.0, 0.0).astype(BF16)
        part = slice(b * LANES, (b + 1) * LANES)
        ext_ref[:, part] = field_ref[:, part] * keep
    ext_ref[:, OWN : OWN + LANES] = jnp.zeros((CH, LANES), BF16)
    for q in range(OWN_WIN):
        win_ref[CH * q : CH * (q + 1), :] = ext_ref[:, STRIDE * q : STRIDE * q + WINDOW]


def gather_kernel(own_ref, north_ref, south_ref, where_ref, out_ref, rim_ref, win_ref, m0, m1, tail_ref):
    rim_ref[:, RIM_OWN + 2 * HALO :] = jnp.zeros((CH, RIM - RIM_OWN - 2 * HALO), BF16)
    rim_ref[:, 0:RIM_OWN] = own_ref[CH * (OWN_WIN - 1) : CH * OWN_WIN, 0:RIM_OWN]
    rim_ref[:, RIM_OWN : RIM_OWN + HALO] = north_ref[...]
    rim_ref[:, RIM_OWN + HALO : RIM_OWN + 2 * HALO] = south_ref[...]
    win_ref[0 : CH * (OWN_WIN - 1), :] = own_ref[0 : CH * (OWN_WIN - 1), :]
    for q in range(OWN_WIN - 1, N_WIN):
        at = STRIDE * (q - OWN_WIN + 1)
        win_ref[CH * q : CH * (q + 1), :] = rim_ref[:, at : at + WINDOW]

    def window_number(start, width):
        index = where_ref[0:1, pl.ds(start, width)].astype(jnp.int32)
        return index, (index * 32897) >> 23

    def make_weights(start, width, m_ref):
        index, number = window_number(start, width)
        frac = where_ref[1:2, pl.ds(start, width)]
        used = index >= 0
        offset = (index - STRIDE * number).astype(F32)
        offset = jnp.broadcast_to(offset, (16, width)).astype(BF16)
        low = jnp.broadcast_to(jnp.where(used, 1.0 - frac, 0.0), (16, width)).astype(BF16)
        high = jnp.broadcast_to(jnp.where(used, frac, 0.0), (16, width)).astype(BF16)
        row16 = lax.broadcasted_iota(jnp.int32, (16, width), 0).astype(F32)
        for s in range(WINDOW // 16):
            row = (row16 + 16.0 * s).astype(BF16)
            before = (row16 + (16.0 * s - 1.0)).astype(BF16)
            m_ref[16 * s : 16 * (s + 1), 0:width] = jnp.where(
                row == offset, low, jnp.where(before == offset, high, jnp.zeros_like(low))
            )

    def choose(start, width, m_ref):
        windows = jnp.dot(win_ref[...], m_ref[:, 0:width], preferred_element_type=F32)
        index, number = window_number(start, width)
        number = jnp.broadcast_to(number, (CH, width))
        bits = [(number & (1 << i)) != 0 for i in range(6)]

        def pick(low, level):
            if level == 0:
                return windows[CH * low : CH * (low + 1)]
            near = pick(low, level - 1)
            far = low + (1 << (level - 1))
            if far >= N_WIN:
                return near
            return jnp.where(bits[level - 1], pick(far, level - 1), near)

        return pick(0, 6)

    def put_main(step, m_ref):
        total = choose(pl.multiple_of(step * BATCH, BATCH), BATCH, m_ref).astype(BF16)
        for i in range(BATCH // LANES):
            out_ref[BATCH // LANES * step + i, 0:CH, :] = total[:, i * LANES : (i + 1) * LANES]

    def weights(step, m_ref):
        make_weights(pl.multiple_of(step * BATCH, BATCH), BATCH, m_ref)

    def main_pair(i, carry):
        weights(2 * i + 1, m1)
        put_main(2 * i, m0)
        weights(2 * i + 2, m0)
        put_main(2 * i + 1, m1)
        return carry

    def tail_pair(i, carry):
        step = MAIN_STEPS + 2 * i
        weights(step + 1, m1)
        at = pl.multiple_of(2 * i * BATCH, BATCH)
        tail_ref[:, pl.ds(at, BATCH)] = choose(pl.multiple_of(step * BATCH, BATCH), BATCH, m0)
        weights(jnp.minimum(step + 2, FULL_STEPS - 1), m0)
        step = step + 1
        at = pl.multiple_of(at + BATCH, BATCH)
        tail_ref[:, pl.ds(at, BATCH)] = choose(pl.multiple_of(step * BATCH, BATCH), BATCH, m1)
        return carry

    weights(0, m0)
    lax.fori_loop(0, MAIN_STEPS // 2, main_pair, 0)
    lax.fori_loop(0, (FULL_STEPS - MAIN_STEPS) // 2, tail_pair, 0)
    rest = FULL_STEPS * BATCH
    make_weights(rest, OWN - rest, m0)
    tail_ref[:, rest - MAIN_COLS :] = choose(rest, OWN - rest, m0)

    left = lane_iota(8) < 64
    for d in range(N_LON):
        at = 2 * TAIL * d
        tile, place = at // LANES, at % LANES
        halves = []
        for h in range(2):
            rows = slice(8 * h, 8 * h + 8)
            here = tail_ref[rows, tile * LANES : (tile + 1) * LANES]
            if place + 2 * TAIL > LANES:
                there = tail_ref[rows, (tile + 1) * LANES : (tile + 2) * LANES]
                here = jnp.where(lane_iota(8) >= place, here, there)
            halves.append(pltpu.roll(here, (64 * h - place) % LANES, 1))
        out_ref[d, CH : CH + 8, :] = jnp.where(left, halves[0], halves[1]).astype(BF16)


def cos_sin(product, length, inverse):
    turns = product - jnp.round(product * inverse) * length
    half = turns * (inverse * math.pi)
    z = half * half
    s = -1.0 / 39916800.0
    for c in (1.0 / 362880.0, -1.0 / 5040.0, 1.0 / 120.0, -1.0 / 6.0, 1.0):
        s = s * z + c
    s = s * half
    c0 = 1.0 / 479001600.0
    for c in (-1.0 / 3628800.0, 1.0 / 40320.0, -1.0 / 720.0, 1.0 / 24.0, -0.5, 1.0):
        c0 = c0 * z + c
    return 1.0 - 2.0 * s * s, 2.0 * s * c0


def rotate(cosine, sine, by_cos, by_sin):
    return cosine * by_cos - sine * by_sin, sine * by_cos + cosine * by_sin


def spectral_kernel(len_ref, diff_ref, in_ref, out_ref, x0, x1, w_ref, base_ref, p_ref, y_ref):
    lon_index = lax.axis_index("lon")
    lengths = [len_ref[0, 2 * lon_index + turn] for turn in range(2)]
    for near in range(NEAR):
        w_ref[LANES * near + SLOT_ROWS : LANES * (near + 1), :] = jnp.zeros(
            (LANES - SLOT_ROWS, 4 * TRUNC), BF16
        )
    left = lane_iota(8) < 64

    def load_step(far, carry):
        at = pl.multiple_of(far * CH, CH)
        for near in range(NEAR):
            l = far * NEAR + near
            main = in_ref[l, 0:CH, :].astype(F32)
            tail = in_ref[l, CH : CH + 8, :].astype(F32)
            swap = pltpu.roll(main, 64, 1)
            first = [
                jnp.where(left, main[0:8], pltpu.roll(tail, 64, 1)),
                jnp.where(left, main[8:16], tail),
            ]
            second = [
                jnp.where(left, swap[0:8], pltpu.roll(tail, HEAD - TAIL, 1)),
                jnp.where(left, swap[8:16], pltpu.roll(tail, LANES - TAIL, 1)),
            ]
            lanes = slice(LANES * near, LANES * (near + 1))
            x0[pl.ds(at, CH), lanes] = jnp.concatenate(first, axis=0).astype(BF16)
            x1[pl.ds(at, CH), lanes] = jnp.concatenate(second, axis=0).astype(BF16)
        return carry

    lax.fori_loop(0, FAR, load_step, 0, unroll=2)

    row = lax.broadcasted_iota(jnp.int32, (CH, LANES), 0)
    diffusion = jnp.zeros((CH, LANES), F32)
    for c in range(CH):
        diffusion = jnp.where(row == c, diff_ref[c], diffusion)

    first_row = lax.broadcasted_iota(jnp.int32, (8, LANES), 0) == 0
    i48 = lax.broadcasted_iota(jnp.int32, (48, LANES), 0)
    factor = jnp.where(
        i48 < 8,
        N_LON * i48,
        jnp.where(i48 < 24, 8 * N_LON * (i48 - 8), jnp.where(i48 < 40, NEAR * (i48 - 24), i48 - 40)),
    ).astype(F32)

    for turn in range(2):
        length_int = lengths[turn]
        x_ref = (x0, x1)[turn]

        def block_step(block, carry, turn=turn, length_int=length_int, x_ref=x_ref):
            length = jnp.full((1, LANES), length_int, jnp.int32).astype(F32)
            inverse = 1.0 / length
            wave = lane_iota(1) + block * LANES
            wave_f = wave.astype(F32)
            column = pl.multiple_of((turn * K_BLOCKS + block) * 2 * LANES, 2 * LANES)
            cosine, sine = cos_sin(factor * wave_f, length, inverse)
            base_ref[:, 0:LANES] = cosine
            base_ref[:, LANES : 2 * LANES] = sine

            def base(i):
                return base_ref[i : i + 1, 0:LANES], base_ref[i : i + 1, LANES : 2 * LANES]

            low_cos, low_sin = cosine[0:8], sine[0:8]
            for pair in range(SLOT_ROWS // 16):
                strips = [rotate(low_cos, low_sin, *base(8 + 2 * pair + h)) for h in range(2)]
                if pair == SLOT_ROWS // 16 - 1:
                    strips[0] = [jnp.where(first_row, v, 0.0) for v in strips[0]]
                    strips[1] = [jnp.zeros_like(v) for v in strips[1]]
                for near in range(NEAR):
                    turned = strips if near == 0 else [rotate(*st, *base(40 + near)) for st in strips]
                    both = jnp.concatenate(
                        [
                            jnp.concatenate([turned[0][0], turned[1][0]], axis=0),
                            jnp.concatenate([turned[0][1], turned[1][1]], axis=0),
                        ],
                        axis=1,
                    )
                    at = LANES * near + 16 * pair
                    w_ref[at : at + 16, pl.ds(column, 2 * LANES)] = both.astype(BF16)
            partial = jnp.dot(
                x_ref[...], w_ref[:, pl.ds(column, 2 * LANES)], preferred_element_type=F32
            )
            coeff_cos = jnp.zeros((CH, LANES), F32)
            coeff_sin = jnp.zeros((CH, LANES), F32)
            for far in range(FAR):
                here = partial[CH * far : CH * (far + 1)]
                far_cos, far_sin = base(24 + far)
                coeff_cos += far_cos * here[:, 0:LANES] - far_sin * here[:, LANES:]
                coeff_sin += far_sin * here[:, 0:LANES] + far_cos * here[:, LANES:]
            ratio = wave_f / TRUNC
            weight = jnp.where((wave == 0) | (2 * wave == length_int), 1.0, 2.0)
            weight = jnp.where(2 * wave <= length_int, weight, 0.0)
            damping = weight / ((1.0 + diffusion * (ratio * ratio)) * length)
            amp_cos = coeff_cos * damping
            amp_sin = coeff_sin * damping
            for far in range(FAR):
                far_cos, far_sin = base(24 + far)
                part = jnp.concatenate(
                    [
                        amp_cos * far_cos + amp_sin * far_sin,
                        amp_sin * far_cos - amp_cos * far_sin,
                    ],
                    axis=1,
                )
                p_ref[CH * far : CH * (far + 1), pl.ds(column, 2 * LANES)] = part.astype(BF16)
            return carry

        lax.fori_loop(0, K_BLOCKS, block_step, 0)
        half = slice(turn * 2 * TRUNC, (turn + 1) * 2 * TRUNC)
        y_ref[turn] = lax.dot_general(
            p_ref[:, half], w_ref[:, half], (((1,), (1,)), ((), ())), preferred_element_type=F32
        )

    lane = lane_iota(8)
    bounds = [lane * N_LON - length_int for length_int in lengths]

    def out_step(far, carry):
        at = pl.multiple_of(far * CH, CH)
        for near in range(NEAR):
            l = far * NEAR + near
            lanes = slice(LANES * near, LANES * (near + 1))
            pieces = []
            for turn in range(2):
                inside = bounds[turn] + l < 0
                here = y_ref[turn, pl.ds(at, CH), lanes]
                pieces.append([jnp.where(inside, here[0:8], 0.0), jnp.where(inside, here[8:16], 0.0)])
            main = [jnp.where(left, pieces[0][h], pltpu.roll(pieces[1][h], 64, 1)) for h in range(2)]
            out_ref[l, 0:CH, :] = jnp.concatenate(main, axis=0).astype(BF16)
            tail = jnp.where(
                lane < TAIL,
                pltpu.roll(pieces[0][0], 64, 1),
                jnp.where(
                    lane < 64,
                    pltpu.roll(pieces[1][0], 64 + TAIL, 1),
                    jnp.where(lane < 64 + TAIL, pieces[0][1], pltpu.roll(pieces[1][1], TAIL, 1)),
                ),
            )
            out_ref[l, CH : CH + 8, :] = tail.astype(BF16)
        return carry

    lax.fori_loop(0, FAR, out_step, 0, unroll=2)


def final_kernel(in_ref, out_ref):
    lane = lane_iota(CH).astype(F32).astype(BF16)
    tiles = {}

    def place(source, source_lane, begin, width):
        tile, lane_at = begin // LANES, begin % LANES
        moved = pltpu.roll(source, (lane_at - source_lane) % LANES, 1)
        if tile in tiles:
            tiles[tile] = jnp.where(lane >= lane_at, moved, tiles[tile])
        else:
            tiles[tile] = moved
        if lane_at + width >= LANES:
            out_ref[:, tile * LANES : (tile + 1) * LANES] = tiles.pop(tile)
            if lane_at + width > LANES:
                tiles[tile + 1] = moved

    for d in range(N_LON):
        main = in_ref[d, 0:CH, :]
        tail = in_ref[d, CH : CH + 8, :].astype(F32)
        tail = jnp.concatenate([tail, pltpu.roll(tail, 64, 1)], axis=0).astype(BF16)
        for turn in range(2):
            begin = SLOTS * (2 * d + turn)
            place(main, HEAD * turn, begin, HEAD)
            place(tail, TAIL * turn, begin + HEAD, TAIL)


def vmem():
    return pl.BlockSpec(memory_space=pltpu.VMEM)


def smem():
    return pl.BlockSpec(memory_space=pltpu.SMEM)


def shape(dims, dtype=BF16):
    return pltpu.VMEM(dims, dtype)


def near(x):
    return pltpu.with_memory_space_constraint(x, pltpu.VMEM)


def exchange(blocks):
    return lax.all_to_all(blocks, "lon", split_axis=0, concat_axis=0, tiled=True)


def on_device(field, dep_frac, dep_index, send_list, send_count, cycle_len, diffusion):
    lon_index = lax.axis_index("lon")
    bands = lax.axis_size("lat")
    toward_before, toward_after = pl.pallas_call(
        pick_kernel,
        out_shape=(shape((CH, HALO)), shape((CH, HALO))),
        in_specs=[smem(), smem(), smem(), vmem()],
        out_specs=(vmem(), vmem()),
        name="pick_blocks",
    )(send_list, send_count, cycle_len, field)
    north = lax.ppermute(toward_after, "lat", [(i, i + 1) for i in range(bands - 1)])
    south = lax.ppermute(toward_before, "lat", [(i + 1, i) for i in range(bands - 1)])

    windows, stencil = pl.pallas_call(
        prepare_kernel,
        out_shape=(shape((CH * OWN_WIN, WINDOW)), shape((2, OWN), F32)),
        in_specs=[smem(), vmem(), vmem(), vmem()],
        out_specs=(vmem(), vmem()),
        scratch_shapes=[
            pltpu.VMEM((CH, OWN + LANES), BF16),
            pltpu.VMEM((8, OWN + LANES), F32),
        ],
        name="prepare",
    )(cycle_len, field, dep_index, dep_frac.reshape(1, OWN))

    departed = pl.pallas_call(
        gather_kernel,
        out_shape=shape((N_LON, CH + 8, LANES)),
        in_specs=[vmem(), vmem(), vmem(), vmem()],
        out_specs=vmem(),
        scratch_shapes=[
            pltpu.VMEM((CH, RIM), BF16),
            pltpu.VMEM((CH * N_WIN, WINDOW), BF16),
            pltpu.VMEM((WINDOW, BATCH), BF16),
            pltpu.VMEM((WINDOW, BATCH), BF16),
            pltpu.VMEM((CH, OWN - MAIN_COLS), F32),
        ],
        name="departure_gather",
    )(near(windows), near(north), near(south), near(stencil))

    received = exchange(departed)

    filtered = pl.pallas_call(
        spectral_kernel,
        out_shape=shape((N_LON, CH + 8, LANES)),
        in_specs=[smem(), smem(), vmem()],
        out_specs=vmem(),
        scratch_shapes=[
            pltpu.VMEM((FAR * CH, NEAR * LANES), BF16),
            pltpu.VMEM((FAR * CH, NEAR * LANES), BF16),
            pltpu.VMEM((NEAR * LANES, 4 * TRUNC), BF16),
            pltpu.VMEM((48, 2 * LANES), F32),
            pltpu.VMEM((FAR * CH, 4 * TRUNC), BF16),
            pltpu.VMEM((2, FAR * CH, NEAR * LANES), F32),
        ],
        name="zonal_filter",
    )(cycle_len, diffusion, near(received))

    landed = exchange(filtered)

    return pl.pallas_call(
        final_kernel,
        out_shape=jax.ShapeDtypeStruct((CH, OWN), BF16),
        in_specs=[vmem()],
        out_specs=vmem(),
        name="unpack_columns",
    )(near(landed))


def solution(mesh):
    placed = (
        P(None, ("lat", "lon")),
        P(("lat", "lon")),
        P(None, ("lat", "lon")),
        P(("lat", "lon"), None, None),
        P(("lat", "lon"), None),
        P("lat", None),
        P(),
    )
    return jax.shard_map(
        on_device, mesh=mesh, in_specs=placed, out_specs=P(None, ("lat", "lon")), check_vma=False
    )
```

time: 176 us -> 78.4 us (0.45)
  the two profiles are of different devices: /device:TPU:512 before, /device:TPU:387 now
where the time goes in v1:
time: 78.4 us; the launch traced here: 78.1 us
  blocking collectives  48.9 us (62%)
  Pallas kernels  17.9 us (23%)
  starting transfers between devices  8.6 us (11%)
  waiting for transfers between devices  2.02 us (3%)
    all_to_all x2, blocking collectives, exchange(): lax.all_to_all(blocks, 'lon', split_axis=0, concat_axis=0, tiled=True)  48.9 us
    ppermute x1, starting transfers between devices, on_device(): lax.ppermute(toward_after, 'lat', [(i, i + 1) for i in range(bands - 1)])  6.68 us
    pallas_call x1, Pallas kernels, on_device(): pl.pallas_call(gather_kernel, out_shape=shape((N_LON, CH + 8, LANES)), in...  6.61 us
    pallas_call x1, Pallas kernels, on_device(): pl.pallas_call(spectral_kernel, out_shape=shape((N_LON, CH + 8, LANES)),...  6.57 us
    ppermute x1, waiting for transfers between devices, on_device(): lax.ppermute(toward_before, 'lat', [(i + 1, i) for i in range(bands - 1)])  2.02 us
    ppermute x1, starting transfers between devices, on_device(): lax.ppermute(toward_before, 'lat', [(i + 1, i) for i in range(bands - 1)])  1.92 us
    pallas_call x1, Pallas kernels, on_device(): pl.pallas_call(final_kernel, out_shape=jax.ShapeDtypeStruct((CH, OWN), BF...  1.8 us
    pallas_call x1, Pallas kernels, on_device(): pl.pallas_call(prepare_kernel, out_shape=(shape((CH * OWN_WIN, WINDOW)),...  1.73 us
  transfers between devices with their start and end apart: 2, of which 1 were waited for; matrix products, arithmetic and copies ran while one was open for 1% of the time, Pallas kernels for 2%

profile of v1, /device:TPU:387, one launch (start us, length us, event | category | flops | bytes accessed | tf_op | source)
XLA Modules:
  0.0 78.1 jit_solution(13147052518665598987)
XLA Ops:
  0.0 0.0 copy-start
  0.0 1.2 %pick_blocks.1 = (bf16[16,648]{1,0:T(8,128)(2,1)S(1)}, bf16[16,648]{1,0:T(8,128)(2,1)S(1)}) custom-call(s32[1,2,8]{2,1,0:T(2,128)} %list_ref.1, s32[1,2]{1,0:T(1,128)} %count_ref.1, s32[1,128]{1,0:T(1,128)} %len_ref.5, bf16[16,10368]{1,0:T(8,128)(2,1)} %field_ref.3), custom_call_target="tpu_custom_call" | custom-call | tf_op jit(solution)/shard_map/pick_blocks/pallas_call | solution.py:426
  1.2 6.7 %collective-permute-start = (bf16[16,648]{1,0:T(8,128)(2,1)S(1)}, bf16[16,648]{1,0:T(8,128)(2,1)S(1)}, u32[]{:S(2)}, u32[]{:S(2)}) collective-permute-start(bf16[16,648]{1,0:T(8,128)(2,1)S(1)} %get-tuple-element.10), channel_id=1, source_target_pairs={{0,64},{64,128},{128,192},{192,256},{256,320},{320,384},{384,448},... | collective-permute-start | bytes 62216 | tf_op jit(solution)/shard_map/ppermute | solution.py:433
  7.9 1.9 %collective-permute-start.1 = (bf16[16,648]{1,0:T(8,128)(2,1)S(1)}, bf16[16,648]{1,0:T(8,128)(2,1)S(1)}, u32[]{:S(2)}, u32[]{:S(2)}) collective-permute-start(bf16[16,648]{1,0:T(8,128)(2,1)S(1)} %get-tuple-element.11), channel_id=1, source_target_pairs={{64,0},{128,64},{192,128},{256,192},{320,256},{384,320},{448,384},... | collective-permute-start | bytes 62216 | tf_op jit(solution)/shard_map/ppermute | solution.py:434
  9.8 0.0 copy-done
  9.8 0.6 reshape.3.frac_ref
  10.5 1.7 %prepare.1 = (bf16[656,256]{1,0:T(8,128)(2,1)S(1)}, f32[2,10368]{1,0:T(2,128)S(1)}) custom-call(s32[1,128]{1,0:T(1,128)} %len_ref.5, bf16[16,10368]{1,0:T(8,128)(2,1)} %field_ref.3, s32[2,10368]{1,0:T(2,128)} %index_ref.1, f32[1,10368]{1,0:T(1,128)} %reshape.3.frac_ref), custom_call_target="tpu_custom_call" | custom-call | tf_op jit(solution)/shard_map/prepare/pallas_call | solution.py:436
  12.2 0.0 collective-permute-done.north_ref
  12.2 2.0 %collective-permute-done.1.south_ref = bf16[16,648]{1,0:T(8,128)(2,1)S(1)} collective-permute-done((bf16[16,648]{1,0:T(8,128)(2,1)S(1)}, bf16[16,648]{1,0:T(8,128)(2,1)S(1)}, u32[]{:S(2)}, u32[]{:S(2)}) %collective-permute-start.1) | collective-permute-done | bytes 20768 | tf_op jit(solution)/shard_map/ppermute | solution.py:434
  14.2 6.6 %departure_gather.1 = bf16[64,24,128]{2,1,0:T(8,128)(2,1)S(1)} custom-call(bf16[656,256]{1,0:T(8,128)(2,1)S(1)} %get-tuple-element.9.own_ref, bf16[16,648]{1,0:T(8,128)(2,1)S(1)} %collective-permute-done.north_ref, bf16[16,648]{1,0:T(8,128)(2,1)S(1)} %collective-permute-done.1.south_ref, f32[2,10368]{1,0:T(2,128)S(1)} %get-tuple-element.12.where_ref), custom_call_target="tpu_custom_call" | custom-call | tf_op jit(solution)/shard_map/departure_gather/pallas_call | solution.py:448
  20.8 27.7 %all_to_all.10.in_ref = bf16[64,24,128]{2,1,0:T(8,128)(2,1)S(1)} all-to-all(bf16[64,24,128]{2,1,0:T(8,128)(2,1)S(1)} %departure_gather.1), channel_id=1, replica_groups=mesh['lat'=16,'lon'=64] {'lon'}, dimensions={0} | all-to-all | bytes 786432 | tf_op jit(solution)/shard_map/all_to_all | solution.py:420
  48.6 6.6 %zonal_filter.1 = bf16[64,24,128]{2,1,0:T(8,128)(2,1)S(1)} custom-call(s32[1,128]{1,0:T(1,128)} %len_ref.5, f32[16]{0:T(128)} %diff_ref.1, bf16[64,24,128]{2,1,0:T(8,128)(2,1)S(1)} %all_to_all.10.in_ref), custom_call_target="tpu_custom_call" | custom-call | tf_op jit(solution)/shard_map/zonal_filter/pallas_call | solution.py:465
  55.1 21.2 %all_to_all.11.in_ref = bf16[64,24,128]{2,1,0:T(8,128)(2,1)S(1)} all-to-all(bf16[64,24,128]{2,1,0:T(8,128)(2,1)S(1)} %zonal_filter.1), channel_id=1, replica_groups=mesh['lat'=16,'lon'=64] {'lon'}, dimensions={0} | all-to-all | bytes 786432 | tf_op jit(solution)/shard_map/all_to_all | solution.py:420
  76.3 1.8 %unpack_columns.1 = bf16[16,10368]{1,0:T(8,128)(2,1)} custom-call(bf16[64,24,128]{2,1,0:T(8,128)(2,1)S(1)} %all_to_all.11.in_ref), custom_call_target="tpu_custom_call" | custom-call | tf_op jit(solution)/shard_map/unpack_columns/pallas_call | solution.py:483
Async XLA Ops:
  0.0 9.8 %copy-start = (f32[10368]{0:T(1024)S(1)}, f32[10368]{0:T(1024)}, u32[]{:S(2)}) copy-start(f32[10368]{0:T(1024)} %param.8) | copy-start | bytes 124420
  1.2 11.0 %collective-permute-start = (bf16[16,648]{1,0:T(8,128)(2,1)S(1)}, bf16[16,648]{1,0:T(8,128)(2,1)S(1)}, u32[]{:S(2)}, u32[]{:S(2)}) collective-permute-start(bf16[16,648]{1,0:T(8,128)(2,1)S(1)} %get-tuple-element.10), channel_id=1, source_target_pairs={{0,64},{64,128},{128,192},{192,256},{256,320},{320,384},{384,448},... | collective-permute-start | bytes 62216 | tf_op jit(solution)/shard_map/ppermute | solution.py:433
  7.9 6.4 %collective-permute-start.1 = (bf16[16,648]{1,0:T(8,128)(2,1)S(1)}, bf16[16,648]{1,0:T(8,128)(2,1)S(1)}, u32[]{:S(2)}, u32[]{:S(2)}) collective-permute-start(bf16[16,648]{1,0:T(8,128)(2,1)S(1)} %get-tuple-element.11), channel_id=1, source_target_pairs={{64,0},{128,64},{192,128},{256,192},{320,256},{384,320},{448,384},... | collective-permute-start | bytes 62216 | tf_op jit(solution)/shard_map/ppermute | solution.py:434

commit v2 on v1

--- a/solution.py
+++ b/solution.py
@@ -31,6 +31,7 @@
 BATCH = 2 * WINDOW
 MAIN_STEPS = MAIN_COLS // BATCH
 FULL_STEPS = OWN // BATCH
+OUT_PARTS = 9
 NEAR = 4
 FAR = N_LON // NEAR
 F32 = jnp.float32
@@ -48,7 +49,8 @@
 def pick_kernel(list_ref, count_ref, len_ref, field_ref, first_ref, second_ref):
     lon_index = lax.axis_index("lon")
     lane = lane_iota(CH, 2 * LANES)
-    for way, out_ref in ((0, first_ref), (1, second_ref)):
+    parity = lax.axis_index("lat") & 1
+    for way, out_ref in ((parity, first_ref), (1 - parity, second_ref)):
         blocks = [jnp.zeros((CH, LANES), F32) for _ in range(7)]
         for k in range(HALO_BLOCKS):
             row = jnp.clip(list_ref[0, way, k], 0, CYCLES - 1)
@@ -69,11 +71,19 @@
         out_ref[:, 5 * LANES : HALO] = blocks[5][:, : HALO - 5 * LANES].astype(BF16)
 
 
-def prepare_kernel(len_ref, field_ref, index_ref, frac_ref, win_ref, where_ref, ext_ref, pair_ref):
+def prepare_kernel(
+    len_ref, diff_ref, field_ref, index_ref, frac_ref, win_ref, where_ref, numbers_ref, ext_ref, pair_ref
+):
     lon_index = lax.axis_index("lon")
+    for turn in range(2):
+        length = jnp.full((1, LANES), len_ref[0, 2 * lon_index + turn], jnp.int32)
+        numbers_ref[CH + turn : CH + turn + 1, :] = length.astype(F32)
+    for c in range(CH):
+        numbers_ref[c : c + 1, :] = jnp.full((1, LANES), diff_ref[c], F32)
     pair_ref[:, OWN:] = jnp.zeros((8, LANES), F32)
     pair_ref[0:1, 0:OWN] = index_ref[0:1, :].astype(F32)
-    pair_ref[1:2, 0:OWN] = frac_ref[...]
+    for b in range(OWN // LANES):
+        pair_ref[1:2, b * LANES : (b + 1) * LANES] = frac_ref[b : b + 1, :]
     lane = lane_iota(8)
     tile = None
     for d in range(N_LON):
@@ -119,11 +129,21 @@
         win_ref[CH * q : CH * (q + 1), :] = ext_ref[:, STRIDE * q : STRIDE * q + WINDOW]
 
 
-def gather_kernel(own_ref, north_ref, south_ref, where_ref, out_ref, rim_ref, win_ref, m0, m1, tail_ref):
+def gather_kernel(own_ref, outer_ref, inner_ref, where_ref, out_ref, rim_ref, win_ref, m0, m1, tail_ref):
     rim_ref[:, RIM_OWN + 2 * HALO :] = jnp.zeros((CH, RIM - RIM_OWN - 2 * HALO), BF16)
     rim_ref[:, 0:RIM_OWN] = own_ref[CH * (OWN_WIN - 1) : CH * OWN_WIN, 0:RIM_OWN]
-    rim_ref[:, RIM_OWN : RIM_OWN + HALO] = north_ref[...]
-    rim_ref[:, RIM_OWN + HALO : RIM_OWN + 2 * HALO] = south_ref[...]
+    even = (lax.axis_index("lat") & 1) == 0
+
+    @pl.when(even)
+    def _():
+        rim_ref[:, RIM_OWN : RIM_OWN + HALO] = outer_ref[...]
+        rim_ref[:, RIM_OWN + HALO : RIM_OWN + 2 * HALO] = inner_ref[...]
+
+    @pl.when(jnp.logical_not(even))
+    def _():
+        rim_ref[:, RIM_OWN : RIM_OWN + HALO] = inner_ref[...]
+        rim_ref[:, RIM_OWN + HALO : RIM_OWN + 2 * HALO] = outer_ref[...]
+
     win_ref[0 : CH * (OWN_WIN - 1), :] = own_ref[0 : CH * (OWN_WIN - 1), :]
     for q in range(OWN_WIN - 1, N_WIN):
         at = STRIDE * (q - OWN_WIN + 1)
@@ -166,35 +186,20 @@
 
         return pick(0, 6)
 
-    def put_main(step, m_ref):
-        total = choose(pl.multiple_of(step * BATCH, BATCH), BATCH, m_ref).astype(BF16)
-        for i in range(BATCH // LANES):
-            out_ref[BATCH // LANES * step + i, 0:CH, :] = total[:, i * LANES : (i + 1) * LANES]
-
-    def weights(step, m_ref):
-        make_weights(pl.multiple_of(step * BATCH, BATCH), BATCH, m_ref)
-
-    def main_pair(i, carry):
-        weights(2 * i + 1, m1)
-        put_main(2 * i, m0)
-        weights(2 * i + 2, m0)
-        put_main(2 * i + 1, m1)
-        return carry
-
-    def tail_pair(i, carry):
-        step = MAIN_STEPS + 2 * i
-        weights(step + 1, m1)
-        at = pl.multiple_of(2 * i * BATCH, BATCH)
-        tail_ref[:, pl.ds(at, BATCH)] = choose(pl.multiple_of(step * BATCH, BATCH), BATCH, m0)
-        weights(jnp.minimum(step + 2, FULL_STEPS - 1), m0)
-        step = step + 1
-        at = pl.multiple_of(at + BATCH, BATCH)
-        tail_ref[:, pl.ds(at, BATCH)] = choose(pl.multiple_of(step * BATCH, BATCH), BATCH, m1)
-        return carry
-
-    weights(0, m0)
-    lax.fori_loop(0, MAIN_STEPS // 2, main_pair, 0)
-    lax.fori_loop(0, (FULL_STEPS - MAIN_STEPS) // 2, tail_pair, 0)
+    buffers = (m0, m1)
+    make_weights(0, BATCH, m0)
+    for step in range(FULL_STEPS):
+        if step + 1 < FULL_STEPS:
+            make_weights((step + 1) * BATCH, BATCH, buffers[(step + 1) % 2])
+        total = choose(step * BATCH, BATCH, buffers[step % 2])
+        if step < MAIN_STEPS:
+            total = total.astype(BF16)
+            for i in range(BATCH // LANES):
+                lanes = slice(i * LANES, (i + 1) * LANES)
+                out_ref[BATCH // LANES * step + i, 0:CH, :] = total[:, lanes]
+        else:
+            at = step * BATCH - MAIN_COLS
+            tail_ref[:, at : at + BATCH] = total
     rest = FULL_STEPS * BATCH
     make_weights(rest, OWN - rest, m0)
     tail_ref[:, rest - MAIN_COLS :] = choose(rest, OWN - rest, m0)
@@ -232,17 +237,17 @@
     return cosine * by_cos - sine * by_sin, sine * by_cos + cosine * by_sin
 
 
-def spectral_kernel(len_ref, diff_ref, in_ref, out_ref, x0, x1, w_ref, base_ref, p_ref, y_ref):
-    lon_index = lax.axis_index("lon")
-    lengths = [len_ref[0, 2 * lon_index + turn] for turn in range(2)]
+def spectral_kernel(numbers_ref, in_ref, out_ref, x0, x1, w_ref, base_ref, p_ref, y_ref):
+    lengths = [numbers_ref[CH + turn : CH + turn + 1, :] for turn in range(2)]
+    diffusion = numbers_ref[0:CH, :]
     for near in range(NEAR):
         w_ref[LANES * near + SLOT_ROWS : LANES * (near + 1), :] = jnp.zeros(
             (LANES - SLOT_ROWS, 4 * TRUNC), BF16
         )
     left = lane_iota(8) < 64
 
-    def load_step(far, carry):
-        at = pl.multiple_of(far * CH, CH)
+    for far in range(FAR):
+        rows = slice(CH * far, CH * (far + 1))
         for near in range(NEAR):
             l = far * NEAR + near
             main = in_ref[l, 0:CH, :].astype(F32)
@@ -257,16 +262,8 @@
                 jnp.where(left, swap[8:16], pltpu.roll(tail, LANES - TAIL, 1)),
             ]
             lanes = slice(LANES * near, LANES * (near + 1))
-            x0[pl.ds(at, CH), lanes] = jnp.concatenate(first, axis=0).astype(BF16)
-            x1[pl.ds(at, CH), lanes] = jnp.concatenate(second, axis=0).astype(BF16)
-        return carry
-
-    lax.fori_loop(0, FAR, load_step, 0, unroll=2)
-
-    row = lax.broadcasted_iota(jnp.int32, (CH, LANES), 0)
-    diffusion = jnp.zeros((CH, LANES), F32)
-    for c in range(CH):
-        diffusion = jnp.where(row == c, diff_ref[c], diffusion)
+            x0[rows, lanes] = jnp.concatenate(first, axis=0).astype(BF16)
+            x1[rows, lanes] = jnp.concatenate(second, axis=0).astype(BF16)
 
     first_row = lax.broadcasted_iota(jnp.int32, (8, LANES), 0) == 0
     i48 = lax.broadcasted_iota(jnp.int32, (48, LANES), 0)
@@ -277,21 +274,21 @@
     ).astype(F32)
 
     for turn in range(2):
-        length_int = lengths[turn]
+        length = lengths[turn]
+        inverse = 1.0 / length
         x_ref = (x0, x1)[turn]
-
-        def block_step(block, carry, turn=turn, length_int=length_int, x_ref=x_ref):
-            length = jnp.full((1, LANES), length_int, jnp.int32).astype(F32)
-            inverse = 1.0 / length
-            wave = lane_iota(1) + block * LANES
-            wave_f = wave.astype(F32)
-            column = pl.multiple_of((turn * K_BLOCKS + block) * 2 * LANES, 2 * LANES)
+        for block in range(K_BLOCKS):
+            wave_f = (lane_iota(1) + block * LANES).astype(F32)
+            base_at = base_ref.at[(turn * K_BLOCKS + block) % 2]
+            columns = slice(
+                (turn * K_BLOCKS + block) * 2 * LANES, (turn * K_BLOCKS + block + 1) * 2 * LANES
+            )
             cosine, sine = cos_sin(factor * wave_f, length, inverse)
-            base_ref[:, 0:LANES] = cosine
-            base_ref[:, LANES : 2 * LANES] = sine
-
-            def base(i):
-                return base_ref[i : i + 1, 0:LANES], base_ref[i : i + 1, LANES : 2 * LANES]
+            base_at[:, 0:LANES] = cosine
+            base_at[:, LANES : 2 * LANES] = sine
+
+            def base(i, base_at=base_at):
+                return base_at[i : i + 1, 0:LANES], base_at[i : i + 1, LANES : 2 * LANES]
 
             low_cos, low_sin = cosine[0:8], sine[0:8]
             for pair in range(SLOT_ROWS // 16):
@@ -309,10 +306,8 @@
                         axis=1,
                     )
                     at = LANES * near + 16 * pair
-                    w_ref[at : at + 16, pl.ds(column, 2 * LANES)] = both.astype(BF16)
-            partial = jnp.dot(
-                x_ref[...], w_ref[:, pl.ds(column, 2 * LANES)], preferred_element_type=F32
-            )
+                    w_ref[at : at + 16, columns] = both.astype(BF16)
+            partial = jnp.dot(x_ref[...], w_ref[:, columns], preferred_element_type=F32)
             coeff_cos = jnp.zeros((CH, LANES), F32)
             coeff_sin = jnp.zeros((CH, LANES), F32)
             for far in range(FAR):
@@ -321,8 +316,8 @@
                 coeff_cos += far_cos * here[:, 0:LANES] - far_sin * here[:, LANES:]
                 coeff_sin += far_sin * here[:, 0:LANES] + far_cos * here[:, LANES:]
             ratio = wave_f / TRUNC
-            weight = jnp.where((wave == 0) | (2 * wave == length_int), 1.0, 2.0)
-            weight = jnp.where(2 * wave <= length_int, weight, 0.0)
+            weight = jnp.where((wave_f == 0.0) | (2.0 * wave_f == length), 1.0, 2.0)
+            weight = jnp.where(2.0 * wave_f <= length, weight, 0.0)
             damping = weight / ((1.0 + diffusion * (ratio * ratio)) * length)
             amp_cos = coeff_cos * damping
             amp_sin = coeff_sin * damping
@@ -335,27 +330,24 @@
                     ],
                     axis=1,
                 )
-                p_ref[CH * far : CH * (far + 1), pl.ds(column, 2 * LANES)] = part.astype(BF16)
-            return carry
-
-        lax.fori_loop(0, K_BLOCKS, block_step, 0)
+                p_ref[CH * far : CH * (far + 1), columns] = part.astype(BF16)
         half = slice(turn * 2 * TRUNC, (turn + 1) * 2 * TRUNC)
         y_ref[turn] = lax.dot_general(
             p_ref[:, half], w_ref[:, half], (((1,), (1,)), ((), ())), preferred_element_type=F32
         )
 
     lane = lane_iota(8)
-    bounds = [lane * N_LON - length_int for length_int in lengths]
-
-    def out_step(far, carry):
-        at = pl.multiple_of(far * CH, CH)
+    bounds = [(lane * N_LON).astype(F32) - length for length in lengths]
+
+    for far in range(FAR):
+        rows = slice(CH * far, CH * (far + 1))
         for near in range(NEAR):
             l = far * NEAR + near
             lanes = slice(LANES * near, LANES * (near + 1))
             pieces = []
             for turn in range(2):
-                inside = bounds[turn] + l < 0
-                here = y_ref[turn, pl.ds(at, CH), lanes]
+                inside = bounds[turn] < float(-l)
+                here = y_ref[turn, rows, lanes]
                 pieces.append([jnp.where(inside, here[0:8], 0.0), jnp.where(inside, here[8:16], 0.0)])
             main = [jnp.where(left, pieces[0][h], pltpu.roll(pieces[1][h], 64, 1)) for h in range(2)]
             out_ref[l, 0:CH, :] = jnp.concatenate(main, axis=0).astype(BF16)
@@ -369,12 +361,15 @@
                 ),
             )
             out_ref[l, CH : CH + 8, :] = tail.astype(BF16)
-        return carry
-
-    lax.fori_loop(0, FAR, out_step, 0, unroll=2)
-
-
-def final_kernel(in_ref, out_ref):
+
+
+def final_kernel(in_ref, out_hbm, out_ref, sems):
+    part_tiles = OWN // LANES // OUT_PARTS
+
+    def part_copy(part):
+        columns = slice(part * part_tiles * LANES, (part + 1) * part_tiles * LANES)
+        return pltpu.make_async_copy(out_ref.at[:, columns], out_hbm.at[:, columns], sems.at[part])
+
     lane = lane_iota(CH).astype(F32).astype(BF16)
     tiles = {}
 
@@ -387,6 +382,8 @@
             tiles[tile] = moved
         if lane_at + width >= LANES:
             out_ref[:, tile * LANES : (tile + 1) * LANES] = tiles.pop(tile)
+            if (tile + 1) % part_tiles == 0:
+                part_copy(tile // part_tiles).start()
             if lane_at + width > LANES:
                 tiles[tile + 1] = moved
 
@@ -398,6 +395,8 @@
             begin = SLOTS * (2 * d + turn)
             place(main, HEAD * turn, begin, HEAD)
             place(tail, TAIL * turn, begin + HEAD, TAIL)
+    for part in range(OUT_PARTS):
+        part_copy(part).wait()
 
 
 def vmem():
@@ -423,27 +422,29 @@
 def on_device(field, dep_frac, dep_index, send_list, send_count, cycle_len, diffusion):
     lon_index = lax.axis_index("lon")
     bands = lax.axis_size("lat")
-    toward_before, toward_after = pl.pallas_call(
+    outward, inward = pl.pallas_call(
         pick_kernel,
         out_shape=(shape((CH, HALO)), shape((CH, HALO))),
         in_specs=[smem(), smem(), smem(), vmem()],
         out_specs=(vmem(), vmem()),
         name="pick_blocks",
     )(send_list, send_count, cycle_len, field)
-    north = lax.ppermute(toward_after, "lat", [(i, i + 1) for i in range(bands - 1)])
-    south = lax.ppermute(toward_before, "lat", [(i + 1, i) for i in range(bands - 1)])
-
-    windows, stencil = pl.pallas_call(
+    pairs = [(i, i + 1) for i in range(1, bands - 1, 2)]
+    from_outer = lax.ppermute(outward, "lat", pairs + [(j, i) for i, j in pairs])
+    pairs = [(i, i + 1) for i in range(0, bands - 1, 2)]
+    from_inner = lax.ppermute(inward, "lat", pairs + [(j, i) for i, j in pairs])
+
+    windows, stencil, numbers = pl.pallas_call(
         prepare_kernel,
-        out_shape=(shape((CH * OWN_WIN, WINDOW)), shape((2, OWN), F32)),
-        in_specs=[smem(), vmem(), vmem(), vmem()],
-        out_specs=(vmem(), vmem()),
+        out_shape=(shape((CH * OWN_WIN, WINDOW)), shape((2, OWN), F32), shape((CH + 8, LANES), F32)),
+        in_specs=[smem(), smem(), vmem(), vmem(), vmem()],
+        out_specs=(vmem(), vmem(), vmem()),
         scratch_shapes=[
             pltpu.VMEM((CH, OWN + LANES), BF16),
             pltpu.VMEM((8, OWN + LANES), F32),
         ],
         name="prepare",
-    )(cycle_len, field, dep_index, dep_frac.reshape(1, OWN))
+    )(cycle_len, diffusion, near(field), dep_index, dep_frac.reshape(OWN // LANES, LANES))
 
     departed = pl.pallas_call(
         gather_kernel,
@@ -458,25 +459,25 @@
             pltpu.VMEM((CH, OWN - MAIN_COLS), F32),
         ],
         name="departure_gather",
-    )(near(windows), near(north), near(south), near(stencil))
+    )(near(windows), near(from_outer), near(from_inner), near(stencil))
 
     received = exchange(departed)
 
     filtered = pl.pallas_call(
         spectral_kernel,
         out_shape=shape((N_LON, CH + 8, LANES)),
-        in_specs=[smem(), smem(), vmem()],
+        in_specs=[vmem(), vmem()],
         out_specs=vmem(),
         scratch_shapes=[
             pltpu.VMEM((FAR * CH, NEAR * LANES), BF16),
             pltpu.VMEM((FAR * CH, NEAR * LANES), BF16),
             pltpu.VMEM((NEAR * LANES, 4 * TRUNC), BF16),
-            pltpu.VMEM((48, 2 * LANES), F32),
+            pltpu.VMEM((2, 48, 2 * LANES), F32),
             pltpu.VMEM((FAR * CH, 4 * TRUNC), BF16),
             pltpu.VMEM((2, FAR * CH, NEAR * LANES), F32),
         ],
         name="zonal_filter",
-    )(cycle_len, diffusion, near(received))
+    )(near(numbers), near(received))
 
     landed = exchange(filtered)
 
@@ -484,7 +485,8 @@
         final_kernel,
         out_shape=jax.ShapeDtypeStruct((CH, OWN), BF16),
         in_specs=[vmem()],
-        out_specs=vmem(),
+        out_specs=pl.BlockSpec(memory_space=pl.ANY),
+        scratch_shapes=[pltpu.VMEM((CH, OWN), BF16), pltpu.SemaphoreType.DMA((OUT_PARTS,))],
         name="unpack_columns",
     )(near(landed))
 

time: 78.4 us -> 71.8 us (0.916)
  the two profiles are of different devices: /device:TPU:387 before, /device:TPU:384 now
where the time goes in v2:
time: 71.8 us; the launch traced here: 71.5 us
  blocking collectives  51.7 us (72%)
  Pallas kernels  11.3 us (16%)
  starting transfers between devices  8.42 us (12%)
    all_to_all x2, blocking collectives, exchange(): lax.all_to_all(blocks, 'lon', split_axis=0, concat_axis=0, tiled=True)  51.7 us
    ppermute x1, starting transfers between devices, on_device(): from_inner = lax.ppermute(inward, 'lat', pairs + [(j, i) for i, j in pairs])  6.5 us
    pallas_call x1, Pallas kernels, on_device(): pl.pallas_call(gather_kernel, out_shape=shape((N_LON, CH + 8, LANES)), in...  4.49 us
    pallas_call x1, Pallas kernels, on_device(): pl.pallas_call(spectral_kernel, out_shape=shape((N_LON, CH + 8, LANES)),...  2.2 us
    ppermute x1, starting transfers between devices, on_device(): lax.ppermute(outward, 'lat', pairs + [(j, i) for i, j in pairs])  1.92 us
    pallas_call x1, Pallas kernels, on_device(): pl.pallas_call(final_kernel, out_shape=jax.ShapeDtypeStruct((CH, OWN), BF...  1.76 us
    pallas_call x1, Pallas kernels, on_device(): pl.pallas_call(prepare_kernel, out_shape=(shape((CH * OWN_WIN, WINDOW)),...  1.62 us
  transfers between devices with their start and end apart: 2, of which 0 were waited for; matrix products, arithmetic and copies ran while one was open for 0% of the time, Pallas kernels for 2%

profile of v2, /device:TPU:384, one launch (start us, length us, event | category | flops | bytes accessed | tf_op | source)
XLA Modules:
  0.0 71.5 jit_solution(8625635015701960971)
XLA Ops:
  0.0 0.0 copy-start
  0.0 1.2 %pick_blocks.1 = (bf16[16,648]{1,0:T(8,128)(2,1)S(1)}, bf16[16,648]{1,0:T(8,128)(2,1)S(1)}) custom-call(s32[1,2,8]{2,1,0:T(2,128)} %list_ref.1, s32[1,2]{1,0:T(1,128)} %count_ref.1, s32[1,128]{1,0:T(1,128)} %len_ref.3, bf16[16,10368]{1,0:T(8,128)(2,1)} %field_ref.3), custom_call_target="tpu_custom_call" | custom-call | tf_op jit(solution)/shard_map/pick_blocks/pallas_call | solution.py:425
  1.2 1.9 %collective-permute-start = (bf16[16,648]{1,0:T(8,128)(2,1)S(1)}, bf16[16,648]{1,0:T(8,128)(2,1)S(1)}, u32[]{:S(2)}, u32[]{:S(2)}) collective-permute-start(bf16[16,648]{1,0:T(8,128)(2,1)S(1)} %get-tuple-element.12), channel_id=1, source_target_pairs={{64,128},{192,256},{320,384},{448,512},{576,640},{704,768},{832,89... | collective-permute-start | bytes 62216 | tf_op jit(solution)/shard_map/ppermute | solution.py:433
  3.2 6.5 %collective-permute-start.1 = (bf16[16,648]{1,0:T(8,128)(2,1)S(1)}, bf16[16,648]{1,0:T(8,128)(2,1)S(1)}, u32[]{:S(2)}, u32[]{:S(2)}) collective-permute-start(bf16[16,648]{1,0:T(8,128)(2,1)S(1)} %get-tuple-element.13), channel_id=1, source_target_pairs={{0,64},{128,192},{256,320},{384,448},{512,576},{640,704},{768,832}... | collective-permute-start | bytes 62216 | tf_op jit(solution)/shard_map/ppermute | solution.py:435
  9.7 0.0 copy-done
  9.7 1.6 %prepare.1 = (bf16[656,256]{1,0:T(8,128)(2,1)S(1)}, f32[2,10368]{1,0:T(2,128)S(1)}, f32[24,128]{1,0:T(8,128)S(1)}) custom-call(s32[1,128]{1,0:T(1,128)} %len_ref.3, f32[16]{0:T(128)} %diff_ref.1, bf16[16,10368]{1,0:T(8,128)(2,1)S(1)} %copy-done, s32[2,10368]{1,0:T(2,128)} %index_ref.1, f32[81,128]{1,0:T(8,128)} %bitcast.1), custom_call_target="tpu_custom_call" | custom-call | tf_op jit(solution)/shard_map/prepare/pallas_call | solution.py:437
  11.3 0.0 collective-permute-done.outer_ref
  11.3 0.0 collective-permute-done.1.inner_ref
  11.3 4.5 %departure_gather.1 = bf16[64,24,128]{2,1,0:T(8,128)(2,1)S(1)} custom-call(bf16[656,256]{1,0:T(8,128)(2,1)S(1)} %get-tuple-element.11.own_ref, bf16[16,648]{1,0:T(8,128)(2,1)S(1)} %collective-permute-done.outer_ref, bf16[16,648]{1,0:T(8,128)(2,1)S(1)} %collective-permute-done.1.inner_ref, f32[2,10368]{1,0:T(2,128)S(1)} %get-tuple-element.14.where_ref), custom_call_target="tpu_custom_call" | custom-call | tf_op jit(solution)/shard_map/departure_gather/pallas_call | solution.py:449
  15.8 30.8 %all_to_all.10.in_ref = bf16[64,24,128]{2,1,0:T(8,128)(2,1)S(1)} all-to-all(bf16[64,24,128]{2,1,0:T(8,128)(2,1)S(1)} %departure_gather.1), channel_id=1, replica_groups=mesh['lat'=16,'lon'=64] {'lon'}, dimensions={0} | all-to-all | bytes 786432 | tf_op jit(solution)/shard_map/all_to_all | solution.py:419
  46.6 2.2 %zonal_filter.1 = bf16[64,24,128]{2,1,0:T(8,128)(2,1)S(1)} custom-call(f32[24,128]{1,0:T(8,128)S(1)} %get-tuple-element.10.numbers_ref, bf16[64,24,128]{2,1,0:T(8,128)(2,1)S(1)} %all_to_all.10.in_ref), custom_call_target="tpu_custom_call" | custom-call | tf_op jit(solution)/shard_map/zonal_filter/pallas_call | solution.py:466
  48.9 20.9 %all_to_all.11.in_ref = bf16[64,24,128]{2,1,0:T(8,128)(2,1)S(1)} all-to-all(bf16[64,24,128]{2,1,0:T(8,128)(2,1)S(1)} %zonal_filter.1), channel_id=1, replica_groups=mesh['lat'=16,'lon'=64] {'lon'}, dimensions={0} | all-to-all | bytes 786432 | tf_op jit(solution)/shard_map/all_to_all | solution.py:419
  69.8 1.8 %unpack_columns.1 = bf16[16,10368]{1,0:T(8,128)(2,1)} custom-call(bf16[64,24,128]{2,1,0:T(8,128)(2,1)S(1)} %all_to_all.11.in_ref), custom_call_target="tpu_custom_call" | custom-call | tf_op jit(solution)/shard_map/unpack_columns/pallas_call | solution.py:484
Async XLA Ops:
  0.0 9.7 %copy-start = (bf16[16,10368]{1,0:T(8,128)(2,1)S(1)}, bf16[16,10368]{1,0:T(8,128)(2,1)}, u32[]{:S(2)}) copy-start(bf16[16,10368]{1,0:T(8,128)(2,1)} %field_ref.3) | copy-start | bytes 995332
  1.2 10.1 %collective-permute-start = (bf16[16,648]{1,0:T(8,128)(2,1)S(1)}, bf16[16,648]{1,0:T(8,128)(2,1)S(1)}, u32[]{:S(2)}, u32[]{:S(2)}) collective-permute-start(bf16[16,648]{1,0:T(8,128)(2,1)S(1)} %get-tuple-element.12), channel_id=1, source_target_pairs={{64,128},{192,256},{320,384},{448,512},{576,640},{704,768},{832,89... | collective-permute-start | bytes 62216 | tf_op jit(solution)/shard_map/ppermute | solution.py:433
  3.2 8.2 %collective-permute-start.1 = (bf16[16,648]{1,0:T(8,128)(2,1)S(1)}, bf16[16,648]{1,0:T(8,128)(2,1)S(1)}, u32[]{:S(2)}, u32[]{:S(2)}) collective-permute-start(bf16[16,648]{1,0:T(8,128)(2,1)S(1)} %get-tuple-element.13), channel_id=1, source_target_pairs={{0,64},{128,192},{256,320},{384,448},{512,576},{640,704},{768,832}... | collective-permute-start | bytes 62216 | tf_op jit(solution)/shard_map/ppermute | solution.py:435

commit v3 on v2

--- a/solution.py
+++ b/solution.py
@@ -46,9 +46,21 @@
     return (length - lon_index + (N_LON - 1)) >> 6
 
 
-def pick_kernel(list_ref, count_ref, len_ref, field_ref, first_ref, second_ref):
+def pick_kernel(
+    list_ref, count_ref, len_ref, diff_ref, len_row, field_ref, index_ref, frac_ref,
+    first_ref, second_ref, field_out, index_out, frac_out, len_out, numbers_ref,
+):
+    len_out[...] = len_row[...]
+    field_out[...] = field_ref[...]
+    index_out[...] = index_ref[...]
+    frac_out[...] = frac_ref[...]
     lon_index = lax.axis_index("lon")
     lane = lane_iota(CH, 2 * LANES)
+    for turn in range(2):
+        length = jnp.full((1, LANES), len_ref[0, 2 * lon_index + turn], jnp.int32)
+        numbers_ref[CH + turn : CH + turn + 1, :] = length.astype(F32)
+    for c in range(CH):
+        numbers_ref[c : c + 1, :] = jnp.full((1, LANES), diff_ref[c], F32)
     parity = lax.axis_index("lat") & 1
     for way, out_ref in ((parity, first_ref), (1 - parity, second_ref)):
         blocks = [jnp.zeros((CH, LANES), F32) for _ in range(7)]
@@ -71,15 +83,9 @@
         out_ref[:, 5 * LANES : HALO] = blocks[5][:, : HALO - 5 * LANES].astype(BF16)
 
 
-def prepare_kernel(
-    len_ref, diff_ref, field_ref, index_ref, frac_ref, win_ref, where_ref, numbers_ref, ext_ref, pair_ref
-):
-    lon_index = lax.axis_index("lon")
-    for turn in range(2):
-        length = jnp.full((1, LANES), len_ref[0, 2 * lon_index + turn], jnp.int32)
-        numbers_ref[CH + turn : CH + turn + 1, :] = length.astype(F32)
-    for c in range(CH):
-        numbers_ref[c : c + 1, :] = jnp.full((1, LANES), diff_ref[c], F32)
+def prepare_kernel(len_ref, field_ref, index_ref, frac_ref, win_ref, where_ref, ext_ref, pair_ref):
+    all_used = slots_used(len_ref[...], lax.axis_index("lon"))
+    used_slots = [jnp.broadcast_to(all_used[:, r : r + 1], (8, LANES)) for r in range(CYCLES)]
     pair_ref[:, OWN:] = jnp.zeros((8, LANES), F32)
     pair_ref[0:1, 0:OWN] = index_ref[0:1, :].astype(F32)
     for b in range(OWN // LANES):
@@ -87,7 +93,7 @@
     lane = lane_iota(8)
     tile = None
     for d in range(N_LON):
-        used = [slots_used(len_ref[0, 2 * d + turn], lon_index) for turn in range(2)]
+        used = used_slots[2 * d : 2 * d + 2]
         begin = 2 * SLOTS * d
         here = jnp.where(
             lane < HEAD,
@@ -112,16 +118,15 @@
                     source += LANES
                     tile = jnp.where(lane < limit - LANES, pair_ref[:, source : source + LANES], -1.0)
 
-    lane = lane_iota(CH)
     for b in range(OWN // LANES):
         first = (LANES * b) // SLOTS
         last = (LANES * b + LANES - 1) // SLOTS
-        limit = SLOTS * last + slots_used(len_ref[0, last], lon_index) - LANES * b
-        limit = jnp.full((CH, LANES), limit, jnp.int32)
+        limit = used_slots[last] + (SLOTS * last - LANES * b)
         for r in range(last - 1, first - 1, -1):
-            here = SLOTS * r + slots_used(len_ref[0, r], lon_index) - LANES * b
+            here = used_slots[r] + (SLOTS * r - LANES * b)
             limit = jnp.where(lane < SLOTS * (r + 1) - LANES * b, here, limit)
-        keep = jnp.where(lane < limit, 1.0, 0.0).astype(BF16)
+        keep = jnp.where(lane < limit, 1.0, 0.0)
+        keep = jnp.concatenate([keep, keep], axis=0).astype(BF16)
         part = slice(b * LANES, (b + 1) * LANES)
         ext_ref[:, part] = field_ref[:, part] * keep
     ext_ref[:, OWN : OWN + LANES] = jnp.zeros((CH, LANES), BF16)
@@ -422,29 +427,46 @@
 def on_device(field, dep_frac, dep_index, send_list, send_count, cycle_len, diffusion):
     lon_index = lax.axis_index("lon")
     bands = lax.axis_size("lat")
-    outward, inward = pl.pallas_call(
+    outward, inward, field_near, index_near, frac_near, len_near, numbers = pl.pallas_call(
         pick_kernel,
-        out_shape=(shape((CH, HALO)), shape((CH, HALO))),
-        in_specs=[smem(), smem(), smem(), vmem()],
-        out_specs=(vmem(), vmem()),
+        out_shape=(
+            shape((CH, HALO)),
+            shape((CH, HALO)),
+            shape((CH, OWN)),
+            shape((2, OWN), jnp.int32),
+            shape((OWN // LANES, LANES), F32),
+            shape((1, CYCLES), jnp.int32),
+            shape((CH + 8, LANES), F32),
+        ),
+        in_specs=[smem()] * 4 + [vmem()] * 4,
+        out_specs=(vmem(),) * 7,
         name="pick_blocks",
-    )(send_list, send_count, cycle_len, field)
+    )(
+        send_list,
+        send_count,
+        cycle_len,
+        diffusion,
+        cycle_len,
+        field,
+        dep_index,
+        dep_frac.reshape(OWN // LANES, LANES),
+    )
     pairs = [(i, i + 1) for i in range(1, bands - 1, 2)]
     from_outer = lax.ppermute(outward, "lat", pairs + [(j, i) for i, j in pairs])
     pairs = [(i, i + 1) for i in range(0, bands - 1, 2)]
     from_inner = lax.ppermute(inward, "lat", pairs + [(j, i) for i, j in pairs])
 
-    windows, stencil, numbers = pl.pallas_call(
+    windows, stencil = pl.pallas_call(
         prepare_kernel,
-        out_shape=(shape((CH * OWN_WIN, WINDOW)), shape((2, OWN), F32), shape((CH + 8, LANES), F32)),
-        in_specs=[smem(), smem(), vmem(), vmem(), vmem()],
-        out_specs=(vmem(), vmem(), vmem()),
+        out_shape=(shape((CH * OWN_WIN, WINDOW)), shape((2, OWN), F32)),
+        in_specs=[vmem(), vmem(), vmem(), vmem()],
+        out_specs=(vmem(), vmem()),
         scratch_shapes=[
             pltpu.VMEM((CH, OWN + LANES), BF16),
             pltpu.VMEM((8, OWN + LANES), F32),
         ],
         name="prepare",
-    )(cycle_len, diffusion, near(field), dep_index, dep_frac.reshape(OWN // LANES, LANES))
+    )(near(len_near), near(field_near), near(index_near), near(frac_near))
 
     departed = pl.pallas_call(
         gather_kernel,

time: 71.8 us -> 71.4 us (level)
    pallas_call x1, Pallas kernels: 1.62 us -> 0.9 us  [on_device(): pl.pallas_call(prepare_kernel, out_shape=(shape((CH * OWN_WIN, WINDOW)),...]
  transfers between devices with their start and end apart: 2 -> 2, of which waited for: 0 -> 0; matrix products, arithmetic and copies ran while one was open for 0% -> 0% of each run, Pallas kernels for 2% -> 1%
where the time goes in v3:
time: 71.4 us; the launch traced here: 71.2 us
  blocking collectives  52 us (73%)
  Pallas kernels  10.6 us (15%)
  starting transfers between devices  8.42 us (12%)
    all_to_all x2, blocking collectives, exchange(): lax.all_to_all(blocks, 'lon', split_axis=0, concat_axis=0, tiled=True)  52 us
    ppermute x1, starting transfers between devices, on_device(): from_inner = lax.ppermute(inward, 'lat', pairs + [(j, i) for i, j in pairs])  6.5 us
    pallas_call x1, Pallas kernels, on_device(): pl.pallas_call(gather_kernel, out_shape=shape((N_LON, CH + 8, LANES)), in...  4.57 us
    pallas_call x1, Pallas kernels, on_device(): pl.pallas_call(spectral_kernel, out_shape=shape((N_LON, CH + 8, LANES)),...  2.2 us
    ppermute x1, starting transfers between devices, on_device(): lax.ppermute(outward, 'lat', pairs + [(j, i) for i, j in pairs])  1.92 us
    pallas_call x1, Pallas kernels, on_device(): pl.pallas_call(final_kernel, out_shape=jax.ShapeDtypeStruct((CH, OWN), BF...  1.76 us
  transfers between devices with their start and end apart: 2, of which 0 were waited for; matrix products, arithmetic and copies ran while one was open for 0% of the time, Pallas kernels for 1%

profile of v3, /device:TPU:384, one launch (start us, length us, event | category | flops | bytes accessed | tf_op | source)
XLA Modules:
  0.0 71.2 jit_solution(3655357754810716444)
XLA Ops:
  0.0 1.2 %pick_blocks.1 = (bf16[16,648]{1,0:T(8,128)(2,1)S(1)}, bf16[16,648]{1,0:T(8,128)(2,1)S(1)}, bf16[16,10368]{1,0:T(8,128)(2,1)S(1)}, s32[2,10368]{1,0:T(2,128)S(1)...) custom-call(s32[1,2,8]{2,1,0:T(2,128)} %list_ref.1, s32[1,2]{1,0:T(1,128)} %count_ref.1, ...), custom_call_target="tpu_custom_call" | custom-call | tf_op jit(solution)/shard_map/pick_blocks/pallas_call | solution.py:430
  1.2 1.9 %collective-permute-start = (bf16[16,648]{1,0:T(8,128)(2,1)S(1)}, bf16[16,648]{1,0:T(8,128)(2,1)S(1)}, u32[]{:S(2)}, u32[]{:S(2)}) collective-permute-start(bf16[16,648]{1,0:T(8,128)(2,1)S(1)} %get-tuple-element.20), channel_id=1, source_target_pairs={{64,128},{192,256},{320,384},{448,512},{576,640},{704,768},{832,89... | collective-permute-start | bytes 62216 | tf_op jit(solution)/shard_map/ppermute | solution.py:455
  3.1 6.5 %collective-permute-start.1 = (bf16[16,648]{1,0:T(8,128)(2,1)S(1)}, bf16[16,648]{1,0:T(8,128)(2,1)S(1)}, u32[]{:S(2)}, u32[]{:S(2)}) collective-permute-start(bf16[16,648]{1,0:T(8,128)(2,1)S(1)} %get-tuple-element.21), channel_id=1, source_target_pairs={{0,64},{128,192},{256,320},{384,448},{512,576},{640,704},{768,832}... | collective-permute-start | bytes 62216 | tf_op jit(solution)/shard_map/ppermute | solution.py:457
  9.7 0.9 %prepare.1 = (bf16[656,256]{1,0:T(8,128)(2,1)S(1)}, f32[2,10368]{1,0:T(2,128)S(1)}) custom-call(s32[1,128]{1,0:T(1,128)S(1)} %get-tuple-element.15.len_ref, bf16[16,10368]{1,0:T(8,128)(2,1)S(1)} %get-tuple-element.16.field_ref, s32[2,10368]{1,0:T(2,128)S(1)} %get-tuple-element.17.index_ref, f32[81,128]{1,0:T(8,128)S(1)} %get-tuple-element.18.frac_ref), custom_call_target="tpu_custom_call" | custom-call | tf_op jit(solution)/shard_map/prepare/pallas_call | solution.py:459
  10.6 0.0 collective-permute-done.outer_ref
  10.6 0.0 collective-permute-done.1.inner_ref
  10.6 4.6 %departure_gather.1 = bf16[64,24,128]{2,1,0:T(8,128)(2,1)S(1)} custom-call(bf16[656,256]{1,0:T(8,128)(2,1)S(1)} %get-tuple-element.19.own_ref, bf16[16,648]{1,0:T(8,128)(2,1)S(1)} %collective-permute-done.outer_ref, bf16[16,648]{1,0:T(8,128)(2,1)S(1)} %collective-permute-done.1.inner_ref, f32[2,10368]{1,0:T(2,128)S(1)} %get-tuple-element.22.where_ref), custom_call_target="tpu_custom_call" | custom-call | tf_op jit(solution)/shard_map/departure_gather/pallas_call | solution.py:471
  15.1 30.9 %all_to_all.10.in_ref = bf16[64,24,128]{2,1,0:T(8,128)(2,1)S(1)} all-to-all(bf16[64,24,128]{2,1,0:T(8,128)(2,1)S(1)} %departure_gather.1), channel_id=1, replica_groups=mesh['lat'=16,'lon'=64] {'lon'}, dimensions={0} | all-to-all | bytes 786432 | tf_op jit(solution)/shard_map/all_to_all | solution.py:424
  46.1 2.2 %zonal_filter.1 = bf16[64,24,128]{2,1,0:T(8,128)(2,1)S(1)} custom-call(f32[24,128]{1,0:T(8,128)S(1)} %get-tuple-element.14.numbers_ref, bf16[64,24,128]{2,1,0:T(8,128)(2,1)S(1)} %all_to_all.10.in_ref), custom_call_target="tpu_custom_call" | custom-call | tf_op jit(solution)/shard_map/zonal_filter/pallas_call | solution.py:488
  48.3 21.1 %all_to_all.11.in_ref = bf16[64,24,128]{2,1,0:T(8,128)(2,1)S(1)} all-to-all(bf16[64,24,128]{2,1,0:T(8,128)(2,1)S(1)} %zonal_filter.1), channel_id=1, replica_groups=mesh['lat'=16,'lon'=64] {'lon'}, dimensions={0} | all-to-all | bytes 786432 | tf_op jit(solution)/shard_map/all_to_all | solution.py:424
  69.4 1.8 %unpack_columns.1 = bf16[16,10368]{1,0:T(8,128)(2,1)} custom-call(bf16[64,24,128]{2,1,0:T(8,128)(2,1)S(1)} %all_to_all.11.in_ref), custom_call_target="tpu_custom_call" | custom-call | tf_op jit(solution)/shard_map/unpack_columns/pallas_call | solution.py:506
Async XLA Ops:
  1.2 9.3 %collective-permute-start = (bf16[16,648]{1,0:T(8,128)(2,1)S(1)}, bf16[16,648]{1,0:T(8,128)(2,1)S(1)}, u32[]{:S(2)}, u32[]{:S(2)}) collective-permute-start(bf16[16,648]{1,0:T(8,128)(2,1)S(1)} %get-tuple-element.20), channel_id=1, source_target_pairs={{64,128},{192,256},{320,384},{448,512},{576,640},{704,768},{832,89... | collective-permute-start | bytes 62216 | tf_op jit(solution)/shard_map/ppermute | solution.py:455
  3.1 7.4 %collective-permute-start.1 = (bf16[16,648]{1,0:T(8,128)(2,1)S(1)}, bf16[16,648]{1,0:T(8,128)(2,1)S(1)}, u32[]{:S(2)}, u32[]{:S(2)}) collective-permute-start(bf16[16,648]{1,0:T(8,128)(2,1)S(1)} %get-tuple-element.21), channel_id=1, source_target_pairs={{0,64},{128,192},{256,320},{384,448},{512,576},{640,704},{768,832}... | collective-permute-start | bytes 62216 | tf_op jit(solution)/shard_map/ppermute | solution.py:457

commit v4 on v3

--- a/solution.py
+++ b/solution.py
@@ -207,21 +207,15 @@
             tail_ref[:, at : at + BATCH] = total
     rest = FULL_STEPS * BATCH
     make_weights(rest, OWN - rest, m0)
-    tail_ref[:, rest - MAIN_COLS :] = choose(rest, OWN - rest, m0)
-
-    left = lane_iota(8) < 64
+    tail_ref[:, rest - MAIN_COLS : OWN - MAIN_COLS] = choose(rest, OWN - rest, m0)
+    tail_ref[:, OWN - MAIN_COLS :] = jnp.zeros((CH, LANES), F32)
+
     for d in range(N_LON):
         at = 2 * TAIL * d
-        tile, place = at // LANES, at % LANES
-        halves = []
         for h in range(2):
-            rows = slice(8 * h, 8 * h + 8)
-            here = tail_ref[rows, tile * LANES : (tile + 1) * LANES]
-            if place + 2 * TAIL > LANES:
-                there = tail_ref[rows, (tile + 1) * LANES : (tile + 2) * LANES]
-                here = jnp.where(lane_iota(8) >= place, here, there)
-            halves.append(pltpu.roll(here, (64 * h - place) % LANES, 1))
-        out_ref[d, CH : CH + 8, :] = jnp.where(left, halves[0], halves[1]).astype(BF16)
+            out_ref[d, CH : CH + 8, 64 * h : 64 * (h + 1)] = tail_ref[
+                8 * h : 8 * h + 8, at : at + 64
+            ].astype(BF16)
 
 
 def cos_sin(product, length, inverse):
@@ -375,31 +369,21 @@
         columns = slice(part * part_tiles * LANES, (part + 1) * part_tiles * LANES)
         return pltpu.make_async_copy(out_ref.at[:, columns], out_hbm.at[:, columns], sems.at[part])
 
-    lane = lane_iota(CH).astype(F32).astype(BF16)
-    tiles = {}
-
-    def place(source, source_lane, begin, width):
-        tile, lane_at = begin // LANES, begin % LANES
-        moved = pltpu.roll(source, (lane_at - source_lane) % LANES, 1)
-        if tile in tiles:
-            tiles[tile] = jnp.where(lane >= lane_at, moved, tiles[tile])
-        else:
-            tiles[tile] = moved
-        if lane_at + width >= LANES:
-            out_ref[:, tile * LANES : (tile + 1) * LANES] = tiles.pop(tile)
-            if (tile + 1) % part_tiles == 0:
-                part_copy(tile // part_tiles).start()
-            if lane_at + width > LANES:
-                tiles[tile + 1] = moved
-
+    started = 0
     for d in range(N_LON):
         main = in_ref[d, 0:CH, :]
-        tail = in_ref[d, CH : CH + 8, :].astype(F32)
-        tail = jnp.concatenate([tail, pltpu.roll(tail, 64, 1)], axis=0).astype(BF16)
+        tail = in_ref[d, CH : CH + 8, :]
         for turn in range(2):
             begin = SLOTS * (2 * d + turn)
-            place(main, HEAD * turn, begin, HEAD)
-            place(tail, TAIL * turn, begin + HEAD, TAIL)
+            out_ref[:, begin : begin + HEAD] = main[:, HEAD * turn : HEAD * (turn + 1)]
+            for half in range(2):
+                lanes = 64 * half + TAIL * turn
+                out_ref[8 * half : 8 * half + 8, begin + HEAD : begin + SLOTS] = tail[
+                    :, lanes : lanes + TAIL
+                ]
+        while started < OUT_PARTS and 2 * SLOTS * (d + 1) >= (started + 1) * part_tiles * LANES:
+            part_copy(started).start()
+            started += 1
     for part in range(OUT_PARTS):
         part_copy(part).wait()
 
@@ -478,7 +462,7 @@
             pltpu.VMEM((CH * N_WIN, WINDOW), BF16),
             pltpu.VMEM((WINDOW, BATCH), BF16),
             pltpu.VMEM((WINDOW, BATCH), BF16),
-            pltpu.VMEM((CH, OWN - MAIN_COLS), F32),
+            pltpu.VMEM((CH, OWN - MAIN_COLS + LANES), F32),
         ],
         name="departure_gather",
     )(near(windows), near(from_outer), near(from_inner), near(stencil))

time: 71.4 us -> 70.8 us (level)
  no operation moved by 1% of the time
where the time goes in v4:
time: 70.8 us; the launch traced here: 70.6 us
  blocking collectives  52 us (73%)
  Pallas kernels  10.1 us (14%)
  starting transfers between devices  8.42 us (12%)
    all_to_all x2, blocking collectives, exchange(): lax.all_to_all(blocks, 'lon', split_axis=0, concat_axis=0, tiled=True)  52 us
    ppermute x1, starting transfers between devices, on_device(): from_inner = lax.ppermute(inward, 'lat', pairs + [(j, i) for i, j in pairs])  6.5 us
    pallas_call x1, Pallas kernels, on_device(): pl.pallas_call(gather_kernel, out_shape=shape((N_LON, CH + 8, LANES)), in...  4.6 us
    pallas_call x1, Pallas kernels, on_device(): pl.pallas_call(spectral_kernel, out_shape=shape((N_LON, CH + 8, LANES)),...  2.2 us
    ppermute x1, starting transfers between devices, on_device(): lax.ppermute(outward, 'lat', pairs + [(j, i) for i, j in pairs])  1.92 us
  transfers between devices with their start and end apart: 2, of which 0 were waited for; matrix products, arithmetic and copies ran while one was open for 0% of the time, Pallas kernels for 1%

profile of v4, /device:TPU:384, one launch (start us, length us, event | category | flops | bytes accessed | tf_op | source)
XLA Modules:
  0.0 70.6 jit_solution(4508288952549196771)
XLA Ops:
  0.0 1.2 %pick_blocks.1 = (bf16[16,648]{1,0:T(8,128)(2,1)S(1)}, bf16[16,648]{1,0:T(8,128)(2,1)S(1)}, bf16[16,10368]{1,0:T(8,128)(2,1)S(1)}, s32[2,10368]{1,0:T(2,128)S(1)...) custom-call(s32[1,2,8]{2,1,0:T(2,128)} %list_ref.1, s32[1,2]{1,0:T(1,128)} %count_ref.1, ...), custom_call_target="tpu_custom_call" | custom-call | tf_op jit(solution)/shard_map/pick_blocks/pallas_call | solution.py:414
  1.2 1.9 %collective-permute-start = (bf16[16,648]{1,0:T(8,128)(2,1)S(1)}, bf16[16,648]{1,0:T(8,128)(2,1)S(1)}, u32[]{:S(2)}, u32[]{:S(2)}) collective-permute-start(bf16[16,648]{1,0:T(8,128)(2,1)S(1)} %get-tuple-element.20), channel_id=1, source_target_pairs={{64,128},{192,256},{320,384},{448,512},{576,640},{704,768},{832,89... | collective-permute-start | bytes 62216 | tf_op jit(solution)/shard_map/ppermute | solution.py:439
  3.1 6.5 %collective-permute-start.1 = (bf16[16,648]{1,0:T(8,128)(2,1)S(1)}, bf16[16,648]{1,0:T(8,128)(2,1)S(1)}, u32[]{:S(2)}, u32[]{:S(2)}) collective-permute-start(bf16[16,648]{1,0:T(8,128)(2,1)S(1)} %get-tuple-element.21), channel_id=1, source_target_pairs={{0,64},{128,192},{256,320},{384,448},{512,576},{640,704},{768,832}... | collective-permute-start | bytes 62216 | tf_op jit(solution)/shard_map/ppermute | solution.py:441
  9.7 0.9 %prepare.1 = (bf16[656,256]{1,0:T(8,128)(2,1)S(1)}, f32[2,10368]{1,0:T(2,128)S(1)}) custom-call(s32[1,128]{1,0:T(1,128)S(1)} %get-tuple-element.15.len_ref, bf16[16,10368]{1,0:T(8,128)(2,1)S(1)} %get-tuple-element.16.field_ref, s32[2,10368]{1,0:T(2,128)S(1)} %get-tuple-element.17.index_ref, f32[81,128]{1,0:T(8,128)S(1)} %get-tuple-element.18.frac_ref), custom_call_target="tpu_custom_call" | custom-call | tf_op jit(solution)/shard_map/prepare/pallas_call | solution.py:443
  10.6 0.0 collective-permute-done.outer_ref
  10.6 0.0 collective-permute-done.1.inner_ref
  10.6 4.6 %departure_gather.1 = bf16[64,24,128]{2,1,0:T(8,128)(2,1)S(1)} custom-call(bf16[656,256]{1,0:T(8,128)(2,1)S(1)} %get-tuple-element.19.own_ref, bf16[16,648]{1,0:T(8,128)(2,1)S(1)} %collective-permute-done.outer_ref, bf16[16,648]{1,0:T(8,128)(2,1)S(1)} %collective-permute-done.1.inner_ref, f32[2,10368]{1,0:T(2,128)S(1)} %get-tuple-element.22.where_ref), custom_call_target="tpu_custom_call" | custom-call | tf_op jit(solution)/shard_map/departure_gather/pallas_call | solution.py:455
  15.2 30.9 %all_to_all.10.in_ref = bf16[64,24,128]{2,1,0:T(8,128)(2,1)S(1)} all-to-all(bf16[64,24,128]{2,1,0:T(8,128)(2,1)S(1)} %departure_gather.1), channel_id=1, replica_groups=mesh['lat'=16,'lon'=64] {'lon'}, dimensions={0} | all-to-all | bytes 786432 | tf_op jit(solution)/shard_map/all_to_all | solution.py:408
  46.1 2.2 %zonal_filter.1 = bf16[64,24,128]{2,1,0:T(8,128)(2,1)S(1)} custom-call(f32[24,128]{1,0:T(8,128)S(1)} %get-tuple-element.14.numbers_ref, bf16[64,24,128]{2,1,0:T(8,128)(2,1)S(1)} %all_to_all.10.in_ref), custom_call_target="tpu_custom_call" | custom-call | tf_op jit(solution)/shard_map/zonal_filter/pallas_call | solution.py:472
  48.3 21.1 %all_to_all.11.in_ref = bf16[64,24,128]{2,1,0:T(8,128)(2,1)S(1)} all-to-all(bf16[64,24,128]{2,1,0:T(8,128)(2,1)S(1)} %zonal_filter.1), channel_id=1, replica_groups=mesh['lat'=16,'lon'=64] {'lon'}, dimensions={0} | all-to-all | bytes 786432 | tf_op jit(solution)/shard_map/all_to_all | solution.py:408
  69.4 1.2 %unpack_columns.1 = bf16[16,10368]{1,0:T(8,128)(2,1)} custom-call(bf16[64,24,128]{2,1,0:T(8,128)(2,1)S(1)} %all_to_all.11.in_ref), custom_call_target="tpu_custom_call" | custom-call | tf_op jit(solution)/shard_map/unpack_columns/pallas_call | solution.py:490
Async XLA Ops:
  1.2 9.3 %collective-permute-start = (bf16[16,648]{1,0:T(8,128)(2,1)S(1)}, bf16[16,648]{1,0:T(8,128)(2,1)S(1)}, u32[]{:S(2)}, u32[]{:S(2)}) collective-permute-start(bf16[16,648]{1,0:T(8,128)(2,1)S(1)} %get-tuple-element.20), channel_id=1, source_target_pairs={{64,128},{192,256},{320,384},{448,512},{576,640},{704,768},{832,89... | collective-permute-start | bytes 62216 | tf_op jit(solution)/shard_map/ppermute | solution.py:439
  3.1 7.4 %collective-permute-start.1 = (bf16[16,648]{1,0:T(8,128)(2,1)S(1)}, bf16[16,648]{1,0:T(8,128)(2,1)S(1)}, u32[]{:S(2)}, u32[]{:S(2)}) collective-permute-start(bf16[16,648]{1,0:T(8,128)(2,1)S(1)} %get-tuple-element.21), channel_id=1, source_target_pairs={{0,64},{128,192},{256,320},{384,448},{512,576},{640,704},{768,832}... | collective-permute-start | bytes 62216 | tf_op jit(solution)/shard_map/ppermute | solution.py:441

commit v5 on v4

--- a/solution.py
+++ b/solution.py
@@ -244,25 +244,20 @@
             (LANES - SLOT_ROWS, 4 * TRUNC), BF16
         )
     left = lane_iota(8) < 64
+    left_half = lane_iota(CH).astype(F32).astype(BF16) < 64.0
 
     for far in range(FAR):
         rows = slice(CH * far, CH * (far + 1))
         for near in range(NEAR):
             l = far * NEAR + near
-            main = in_ref[l, 0:CH, :].astype(F32)
+            main = in_ref[l, 0:CH, :]
             tail = in_ref[l, CH : CH + 8, :].astype(F32)
-            swap = pltpu.roll(main, 64, 1)
-            first = [
-                jnp.where(left, main[0:8], pltpu.roll(tail, 64, 1)),
-                jnp.where(left, main[8:16], tail),
-            ]
-            second = [
-                jnp.where(left, swap[0:8], pltpu.roll(tail, HEAD - TAIL, 1)),
-                jnp.where(left, swap[8:16], pltpu.roll(tail, LANES - TAIL, 1)),
-            ]
+            first = jnp.concatenate([pltpu.roll(tail, 64, 1), tail], axis=0).astype(BF16)
+            second = [pltpu.roll(tail, HEAD - TAIL, 1), pltpu.roll(tail, LANES - TAIL, 1)]
+            second = jnp.concatenate(second, axis=0).astype(BF16)
             lanes = slice(LANES * near, LANES * (near + 1))
-            x0[rows, lanes] = jnp.concatenate(first, axis=0).astype(BF16)
-            x1[rows, lanes] = jnp.concatenate(second, axis=0).astype(BF16)
+            x0[rows, lanes] = jnp.where(left_half, main, first)
+            x1[rows, lanes] = jnp.where(left_half, pltpu.roll(main, 64, 1), second)
 
     first_row = lax.broadcasted_iota(jnp.int32, (8, LANES), 0) == 0
     i48 = lax.broadcasted_iota(jnp.int32, (48, LANES), 0)

time: 70.8 us -> 70.8 us (level)
  no operation moved by 1% of the time
where the time goes in v5:
time: 70.8 us; the launch traced here: 70.6 us
  blocking collectives  52 us (73%)
  Pallas kernels  10.1 us (14%)
  starting transfers between devices  8.42 us (12%)
    all_to_all x2, blocking collectives, exchange(): lax.all_to_all(blocks, 'lon', split_axis=0, concat_axis=0, tiled=True)  52 us
    ppermute x1, starting transfers between devices, on_device(): from_inner = lax.ppermute(inward, 'lat', pairs + [(j, i) for i, j in pairs])  6.5 us
    pallas_call x1, Pallas kernels, on_device(): pl.pallas_call(gather_kernel, out_shape=shape((N_LON, CH + 8, LANES)), in...  4.6 us
    pallas_call x1, Pallas kernels, on_device(): pl.pallas_call(spectral_kernel, out_shape=shape((N_LON, CH + 8, LANES)),...  2.19 us
    ppermute x1, starting transfers between devices, on_device(): lax.ppermute(outward, 'lat', pairs + [(j, i) for i, j in pairs])  1.92 us
  transfers between devices with their start and end apart: 2, of which 0 were waited for; matrix products, arithmetic and copies ran while one was open for 0% of the time, Pallas kernels for 1%

profile of v5, /device:TPU:384, one launch (start us, length us, event | category | flops | bytes accessed | tf_op | source)
XLA Modules:
  0.0 70.6 jit_solution(8235728779336507815)
XLA Ops:
  0.0 1.2 %pick_blocks.1 = (bf16[16,648]{1,0:T(8,128)(2,1)S(1)}, bf16[16,648]{1,0:T(8,128)(2,1)S(1)}, bf16[16,10368]{1,0:T(8,128)(2,1)S(1)}, s32[2,10368]{1,0:T(2,128)S(1)...) custom-call(s32[1,2,8]{2,1,0:T(2,128)} %list_ref.1, s32[1,2]{1,0:T(1,128)} %count_ref.1, ...), custom_call_target="tpu_custom_call" | custom-call | tf_op jit(solution)/shard_map/pick_blocks/pallas_call | solution.py:409
  1.2 1.9 %collective-permute-start = (bf16[16,648]{1,0:T(8,128)(2,1)S(1)}, bf16[16,648]{1,0:T(8,128)(2,1)S(1)}, u32[]{:S(2)}, u32[]{:S(2)}) collective-permute-start(bf16[16,648]{1,0:T(8,128)(2,1)S(1)} %get-tuple-element.20), channel_id=1, source_target_pairs={{64,128},{192,256},{320,384},{448,512},{576,640},{704,768},{832,89... | collective-permute-start | bytes 62216 | tf_op jit(solution)/shard_map/ppermute | solution.py:434
  3.1 6.5 %collective-permute-start.1 = (bf16[16,648]{1,0:T(8,128)(2,1)S(1)}, bf16[16,648]{1,0:T(8,128)(2,1)S(1)}, u32[]{:S(2)}, u32[]{:S(2)}) collective-permute-start(bf16[16,648]{1,0:T(8,128)(2,1)S(1)} %get-tuple-element.21), channel_id=1, source_target_pairs={{0,64},{128,192},{256,320},{384,448},{512,576},{640,704},{768,832}... | collective-permute-start | bytes 62216 | tf_op jit(solution)/shard_map/ppermute | solution.py:436
  9.7 0.9 %prepare.1 = (bf16[656,256]{1,0:T(8,128)(2,1)S(1)}, f32[2,10368]{1,0:T(2,128)S(1)}) custom-call(s32[1,128]{1,0:T(1,128)S(1)} %get-tuple-element.15.len_ref, bf16[16,10368]{1,0:T(8,128)(2,1)S(1)} %get-tuple-element.16.field_ref, s32[2,10368]{1,0:T(2,128)S(1)} %get-tuple-element.17.index_ref, f32[81,128]{1,0:T(8,128)S(1)} %get-tuple-element.18.frac_ref), custom_call_target="tpu_custom_call" | custom-call | tf_op jit(solution)/shard_map/prepare/pallas_call | solution.py:438
  10.6 0.0 collective-permute-done.outer_ref
  10.6 0.0 collective-permute-done.1.inner_ref
  10.6 4.6 %departure_gather.1 = bf16[64,24,128]{2,1,0:T(8,128)(2,1)S(1)} custom-call(bf16[656,256]{1,0:T(8,128)(2,1)S(1)} %get-tuple-element.19.own_ref, bf16[16,648]{1,0:T(8,128)(2,1)S(1)} %collective-permute-done.outer_ref, bf16[16,648]{1,0:T(8,128)(2,1)S(1)} %collective-permute-done.1.inner_ref, f32[2,10368]{1,0:T(2,128)S(1)} %get-tuple-element.22.where_ref), custom_call_target="tpu_custom_call" | custom-call | tf_op jit(solution)/shard_map/departure_gather/pallas_call | solution.py:450
  15.2 30.9 %all_to_all.10.in_ref = bf16[64,24,128]{2,1,0:T(8,128)(2,1)S(1)} all-to-all(bf16[64,24,128]{2,1,0:T(8,128)(2,1)S(1)} %departure_gather.1), channel_id=1, replica_groups=mesh['lat'=16,'lon'=64] {'lon'}, dimensions={0} | all-to-all | bytes 786432 | tf_op jit(solution)/shard_map/all_to_all | solution.py:403
  46.1 2.2 %zonal_filter.1 = bf16[64,24,128]{2,1,0:T(8,128)(2,1)S(1)} custom-call(f32[24,128]{1,0:T(8,128)S(1)} %get-tuple-element.14.numbers_ref, bf16[64,24,128]{2,1,0:T(8,128)(2,1)S(1)} %all_to_all.10.in_ref), custom_call_target="tpu_custom_call" | custom-call | tf_op jit(solution)/shard_map/zonal_filter/pallas_call | solution.py:467
  48.3 21.1 %all_to_all.11.in_ref = bf16[64,24,128]{2,1,0:T(8,128)(2,1)S(1)} all-to-all(bf16[64,24,128]{2,1,0:T(8,128)(2,1)S(1)} %zonal_filter.1), channel_id=1, replica_groups=mesh['lat'=16,'lon'=64] {'lon'}, dimensions={0} | all-to-all | bytes 786432 | tf_op jit(solution)/shard_map/all_to_all | solution.py:403
  69.4 1.2 %unpack_columns.1 = bf16[16,10368]{1,0:T(8,128)(2,1)} custom-call(bf16[64,24,128]{2,1,0:T(8,128)(2,1)S(1)} %all_to_all.11.in_ref), custom_call_target="tpu_custom_call" | custom-call | tf_op jit(solution)/shard_map/unpack_columns/pallas_call | solution.py:485
Async XLA Ops:
  1.2 9.3 %collective-permute-start = (bf16[16,648]{1,0:T(8,128)(2,1)S(1)}, bf16[16,648]{1,0:T(8,128)(2,1)S(1)}, u32[]{:S(2)}, u32[]{:S(2)}) collective-permute-start(bf16[16,648]{1,0:T(8,128)(2,1)S(1)} %get-tuple-element.20), channel_id=1, source_target_pairs={{64,128},{192,256},{320,384},{448,512},{576,640},{704,768},{832,89... | collective-permute-start | bytes 62216 | tf_op jit(solution)/shard_map/ppermute | solution.py:434
  3.1 7.4 %collective-permute-start.1 = (bf16[16,648]{1,0:T(8,128)(2,1)S(1)}, bf16[16,648]{1,0:T(8,128)(2,1)S(1)}, u32[]{:S(2)}, u32[]{:S(2)}) collective-permute-start(bf16[16,648]{1,0:T(8,128)(2,1)S(1)} %get-tuple-element.21), channel_id=1, source_target_pairs={{0,64},{128,192},{256,320},{384,448},{512,576},{640,704},{768,832}... | collective-permute-start | bytes 62216 | tf_op jit(solution)/shard_map/ppermute | solution.py:436
